TPU v7x, 768 devices: a whole 4x8x12 slice. The times are simulated.
768 devices in a mesh: fsdp: 96 (over z, x, core), tensor: 8 (over y).
Axes of the slice: x: 4, y: 8, z: 12, core: 2. Of those that a mesh axis runs over, the one named last changes fastest.
Arguments:
- momentum: float32 [23040, 6144], P('fsdp', 'tensor'), may hold values from -100 to 100
- gradient: bfloat16 [23040, 6144], P('fsdp', 'tensor'), may hold values from -3 to 3
- right_basis: float32 [6144, 512], P('tensor'), may hold values from -0.078125 to 0.078125
Outputs:
- update: bfloat16 [23040, 6144], P('fsdp', 'tensor')
- new_momentum: float32 [23040, 6144], P('fsdp', 'tensor')
- left_scaled: float32 [23040, 512], P('fsdp')
- next_basis: float32 [6144, 512], P(('tensor', 'fsdp'))
All inputs are finite; a program needn't handle non-finite values.
Results may differ from a plain program's by a relative error of at most 0.001.
Values sent between devices are 32-bit elements; how exact they have to be, the bound alone decides.
A program may use at most 32 MiB of HBM per device.

v0:
```python
import math

import jax
import jax.numpy as jnp
from jax import lax
from jax.sharding import PartitionSpec as P

epsilon = 1e-06


def block_norms(right_full):
    squares = lax.psum(jnp.sum(right_full * right_full, axis=0), "tensor")
    return jnp.sqrt(squares + epsilon)


def planes_for(left, scaled_left, right_rows):
    highest = lax.Precision.HIGHEST
    product = jnp.dot(left, right_rows.T, precision=highest)
    update = jnp.dot(scaled_left, right_rows.T, precision=highest)
    return jnp.stack((product, update))


def on_device(momentum, gradient, right_basis):
    highest = lax.Precision.HIGHEST
    summed = momentum + gradient.astype(jnp.float32)
    left_part = jnp.dot(summed, right_basis, precision=highest)
    left_raw = lax.psum(left_part, "tensor")
    gram = lax.psum(jnp.dot(left_raw.T, left_raw, precision=highest), "fsdp")
    factor_lower = jnp.linalg.cholesky(gram)
    left = jax.scipy.linalg.solve_triangular(factor_lower, left_raw.T, lower=True).T
    groups = lax.axis_size("fsdp")
    total_rows = left.shape[0] * groups
    total_cols = summed.shape[1] * lax.axis_size("tensor")
    factor = math.sqrt(total_rows / total_cols)
    right_rows = lax.psum_scatter(
        jnp.dot(summed.T, left, precision=highest), "fsdp", scatter_dimension=0, tiled=True
    )
    right_full = lax.all_gather(right_rows, "fsdp", axis=0, tiled=True)
    column_norm = block_norms(right_full)
    scaled_left = left * (factor / column_norm)[None, :]
    planes = planes_for(left, scaled_left, right_full)
    product = planes[0]
    update = planes[1].astype(jnp.bfloat16)
    new_momentum = summed - 0.5 * product
    next_basis = right_rows / column_norm[None, :]
    return (update, new_momentum, left * math.sqrt(total_rows), next_basis)


def solution(mesh):
    in_specs = (P("fsdp", "tensor"), P("fsdp", "tensor"), P("tensor", None))
    out_specs = (
        P("fsdp", "tensor"),
        P("fsdp", "tensor"),
        P("fsdp", None),
        P(("tensor", "fsdp"), None),
    )
    return jax.shard_map(
        on_device, mesh=mesh, in_specs=in_specs, out_specs=out_specs, check_vma=False
    )
```

profile of v0, /device:TPU:1, one launch (start us, length us, event | category | flops | bytes accessed | tf_op | source)
XLA Modules:
  0.0 899.5 jit_solution(5369049786399800156)
XLA Ops:
  8.6 3.4 fusion.9
  12.1 87.9 %all-reduce.4.cloned.1.call-done = f32[240,512]{1,0:T(8,128)} async-done(((f32[240,512]{1,0:T(8,128)}), f32[240,512]{1,0:T(8,128)}) %all-reduce.4.cloned.1.call-update) | async-done | bytes 491536 | tf_op jit(solution)/shard_map/psum | solution.py:27
  100.0 3.3 fusion.36
  103.8 281.9 %all-reduce.6.cloned.1.call-done = f32[512,512]{0,1:T(8,128)} async-done(((f32[512,512]{0,1:T(8,128)}), f32[512,512]{0,1:T(8,128)}) %all-reduce.6.cloned.1.call-update) | async-done | bytes 1048592 | tf_op jit(solution)/shard_map/psum | solution.py:28
  385.7 2.7 copy.8
  390.9 11.7 %cholesky.104 = f32[128,128]{1,0:T(8,128)S(1)} custom-call(f32[128,128]{1,0:T(8,128)S(1)} %cholesky.266), custom_call_target="Cholesky" | custom-call | tf_op jit(solution)/shard_map/jit(cholesky)/cholesky | solution.py:29
  402.6 9.8 %custom-call.31 = f32[1,128,128]{1,2,0:T(8,128)S(1)} custom-call(f32[1,128,128]{2,1,0:T(8,128)S(1)} %get-tuple-element.31), custom_call_target="InvertDiagBlocksLowerTriangular" | custom-call | tf_op jit(solution)/shard_map/jit(cholesky)/cholesky | solution.py:29
  415.1 11.7 %cholesky.217 = f32[128,128]{1,0:T(8,128)S(1)} custom-call(f32[128,128]{1,0:T(8,128)S(1)} %cholesky.270), custom_call_target="Cholesky" | custom-call | tf_op jit(solution)/shard_map/jit(cholesky)/cholesky | solution.py:29
  426.8 10.0 %custom-call.32 = f32[1,128,128]{1,2,0:T(8,128)S(1)} custom-call(f32[1,128,128]{2,1,0:T(8,128)S(1)} %get-tuple-element.28), custom_call_target="InvertDiagBlocksLowerTriangular" | custom-call | tf_op jit(solution)/shard_map/jit(cholesky)/cholesky | solution.py:29
  438.4 11.7 %cholesky.238 = f32[128,128]{1,0:T(8,128)S(1)} custom-call(f32[128,128]{1,0:T(8,128)S(1)} %cholesky.275), custom_call_target="Cholesky" | custom-call | tf_op jit(solution)/shard_map/jit(cholesky)/cholesky | solution.py:29
  450.8 9.8 %custom-call.33 = f32[1,128,128]{1,2,0:T(8,128)S(1)} custom-call(f32[1,128,128]{2,1,0:T(8,128)S(1)} %get-tuple-element.25), custom_call_target="InvertDiagBlocksLowerTriangular" | custom-call | tf_op jit(solution)/shard_map/jit(cholesky)/cholesky | solution.py:29
  462.1 11.7 %cholesky.255 = f32[128,128]{1,0:T(8,128)S(1)} custom-call(f32[128,128]{1,0:T(8,128)S(1)} %convolution_subtract_fusion.5), custom_call_target="Cholesky" | custom-call | tf_op jit(solution)/shard_map/jit(cholesky)/cholesky | solution.py:29
  479.0 14.0 %while.1 = (s32[]{:T(128)}, f32[512,512]{1,0:T(8,128)}, s32[4,2]{0,1:T(2,128)S(1)}, f32[4,128,128]{2,1,0:T(8,128)}, s32[]{:T(128)}) while((s32[]{:T(128)}, f32[512,512]{1,0:T(8,128)}, s32[4,2]{0,1:T(2,128)S(1)}, f32[4,128,128]{2,1,0:T(8,128)}, s32[]{:T(128)}) %tuple.32), condition=%wide.while_cond, body=%wide.while_body.sunk | while | flops 2 | bytes 132705 | solution.py:30
  479.6 2.9 bitcast_dynamic-update-slice_fusion.2
  483.1 2.9 bitcast_dynamic-update-slice_fusion.2
  486.6 2.9 bitcast_dynamic-update-slice_fusion.2
  490.2 2.9 bitcast_dynamic-update-slice_fusion.2
  493.0 40.8 %custom-call.34 = f32[4,128,128]{1,2,0:T(8,128)} custom-call(f32[4,128,128]{2,1,0:T(8,128)} %get-tuple-element.11), custom_call_target="InvertDiagBlocksLowerTriangular" | custom-call | tf_op jit(solution)/shard_map/jit(_solve_triangular)/triangular_solve | solution.py:30
  540.5 2.7 fusion.8
  543.3 202.1 %reduce-scatter.2.cloned.1.call-done = f32[8,512]{1,0:T(8,128)} async-done(((f32[768,512]{1,0:T(8,128)}), f32[8,512]{1,0:T(8,128)}) %reduce-scatter.2.cloned.1.call-update) | async-done | bytes 16400 | tf_op jit(solution)/shard_map/reduce_scatter | solution.py:35
  746.3 124.8 %all-gather.2.cloned.1.call-done = f32[768,512]{1,0:T(8,128)} async-done(((f32[8,512]{1,0:T(8,128)}), f32[768,512]{1,0:T(8,128)}) %all-gather.2.cloned.1.call-update) | async-done | bytes 1572880 | tf_op jit(solution)/shard_map/all_gather | solution.py:38
  872.7 13.5 %psum.23 = f32[512]{0:T(512)S(1)} all-reduce(f32[512]{0:T(512)S(1)} %multiply_reduce_fusion), channel_id=1, replica_groups=mesh['fsdp'=96,'tensor'=8] {'tensor'}, use_global_device_ids=true, to_apply=%region_12.13 | all-reduce | flops 512 | bytes 4096 | tf_op jit(solution)/shard_map/psum | solution.py:12
  886.3 3.6 fusion
  890.6 2.2 convolution_convert_fusion
  (71 shorter events, 25.7 us)
Async XLA Ops:
  7.2 1.4 copy-start
  7.2 92.8 %all-reduce.4.cloned.1.call-start = ((), (), s32[]{:S(2)}) async-start(), calls=%async_computation.1 | async-start | bytes 983040 | tf_op jit(solution)/shard_map/psum | solution.py:27
  12.0 373.7 %all-reduce.6.cloned.1.call-start = ((), (), s32[]{:S(2)}) async-start(), calls=%async_computation.2 | async-start | bytes 2097152 | tf_op jit(solution)/shard_map/psum | solution.py:28
  103.3 642.1 %reduce-scatter.2.cloned.1.call-start = ((), (), s32[]{:S(2)}) async-start(), calls=%async_computation.3 | async-start | bytes 1589248 | tf_op jit(solution)/shard_map/reduce_scatter | solution.py:35
  385.7 2.7 copy-start.4
  389.9 1.0 copy-start.8
  462.1 71.8 %copy-start.3 = (f32[240,512]{1,0:T(8,128)S(1)}, f32[240,512]{1,0:T(8,128)}, u32[]{:S(2)}) copy-start(f32[240,512]{1,0:T(8,128)} %all-reduce.4.cloned.1.call-done) | copy-start | bytes 1474564
  493.0 47.5 %copy-start.2 = (f32[240,768]{1,0:T(8,128)S(1)}, f32[240,768]{1,0:T(8,128)}, u32[]{:S(2)}) copy-start(f32[240,768]{1,0:T(8,128)} %param.3) | copy-start | bytes 2211844
  493.0 47.5 %copy-start.5 = (bf16[240,768]{1,0:T(8,128)(2,1)S(1)}, bf16[240,768]{1,0:T(8,128)(2,1)}, u32[]{:S(2)}) copy-start(bf16[240,768]{1,0:T(8,128)(2,1)} %param.4) | copy-start | bytes 1105924
  533.9 4.7 copy-start.9
  540.5 204.9 %copy-start.6 = (f32[128,240]{0,1:T(8,128)}, f32[128,240]{0,1:T(8,128)S(1)}, u32[]{:S(2)}) copy-start(f32[128,240]{0,1:T(8,128)S(1)} %fusion.24) | copy-start | bytes 368644
  543.2 327.8 %all-gather.2.cloned.1.call-start = ((), (), s32[]{:S(2)}) async-start(), calls=%async_computation.4 | async-start | bytes 1589248 | tf_op jit(solution)/shard_map/all_gather | solution.py:38
  871.1 15.2 %copy-start.1 = (f32[768,512]{1,0:T(8,128)S(1)}, f32[768,512]{1,0:T(8,128)}, u32[]{:S(2)}) copy-start(f32[768,512]{1,0:T(8,128)} %all-gather.2.cloned.1.call-done) | copy-start | bytes 4718596
  886.3 3.7 copy-start.10
  886.3 4.3 copy-start.7
Sparse Core Ops, SparseCore 0:
  12.2 87.7 all-reduce.3
  103.5 282.1 all-reduce.5
  543.3 202.0 reduce-scatter.1
  748.9 122.0 all-gather.1
where the time goes:
time: 905 us; the launch traced here: 900 us
  waiting for transfers between devices  697 us (77%)
  other arithmetic  125 us (14%)
  matrix products  27.3 us (3%)
  local copies, waits for them, and re-layouts  19.2 us (2%)
  between operations  16.8 us (2%)
  blocking collectives  13.5 us (1%)
    psum x1, waiting for transfers between devices, on_device(): gram = lax.psum(jnp.dot(left_raw.T, left_raw, precision=highest), 'fsdp')  282 us
    reduce_scatter x1, waiting for transfers between devices, on_device(): lax.psum_scatter(jnp.dot(summed.T, left, precision=highest), 'fsdp', scat...  202 us
    all_gather x1, waiting for transfers between devices, on_device(): right_full = lax.all_gather(right_rows, 'fsdp', axis=0, tiled=True)  125 us
    psum x1, waiting for transfers between devices, on_device(): left_raw = lax.psum(left_part, 'tensor')  87.9 us
    another operation x14, other arithmetic, on_device(): factor_lower = jnp.linalg.cholesky(gram)  78.6 us
    another operation x3, other arithmetic, on_device(): jax.scipy.linalg.solve_triangular(factor_lower, left_raw.T, lower=True)  42.2 us
  transfers between devices with their start and end apart: 4, of which 4 were waited for; matrix products, arithmetic and copies ran while one was open for 0% of the time, Pallas kernels for 0%

commit v1 on v0

v1 whole, which is shorter than its diff:
```python
import functools
import math

import jax
import jax.numpy as jnp
from jax import lax
from jax.experimental import pallas as pl
from jax.experimental.pallas import tpu as pltpu
from jax.sharding import PartitionSpec as P

EPSILON = 1e-06
HIGHEST = lax.Precision.HIGHEST
MESH = pl.DeviceIdType.MESH
XS, CORES = 4, 2
VMEM_LIMIT = 60 * 1024 * 1024


def dot(a, b, lhs=1, rhs=0):
    return lax.dot_general(
        a, b, (((lhs,), (rhs,)), ((), ())), precision=HIGHEST, preferred_element_type=jnp.float32
    )


def place():
    f = lax.axis_index("fsdp")
    y = lax.axis_index("tensor")
    return f // (XS * CORES), (f // CORES) % XS, f % CORES, y


def device(z, x, core, y):
    return ((z * XS + x) * CORES + core, y)


def each(start, stop, body):
    def step(i, carry):
        body(i)
        return carry

    lax.fori_loop(start, stop, step, 0)


def reduce_kernel(
    zs_n, ys_n, m_ref, g_ref, q_ref, a_ref, w_ref, gram_ref,
    part, ybuf, chunks, wpart, gpart, cbuf, xsum, xbuf, zsum, zbuf, zgbuf, wfull, gfull,
    s_y, r_y, s_y2, r_y2, s_c, r_c, s_x, r_x, s_z, r_z, s_zg, r_zg, s_gy, r_gy, s_gx, r_gx, s_gc, r_gc,
    s_wz, r_wz, s_wx, r_wx, s_wc, r_wc,
):
    z, x, core, y = place()
    half = part.shape[1]
    lanes = part.shape[2]
    across = a_ref.shape[1] // lanes

    def send(src, dst, ssem, rsem, to):
        pltpu.make_async_remote_copy(
            src_ref=src, dst_ref=dst, send_sem=ssem, recv_sem=rsem, device_id=to, device_id_type=MESH
        ).start()

    def sent(src, ssem):
        pltpu.make_async_copy(src, src, ssem).wait()

    def came(dst, rsem):
        pltpu.make_async_copy(dst, dst, rsem).wait()

    barrier = pltpu.get_barrier_semaphore()

    def greet(to):
        pl.semaphore_signal(barrier, inc=1, device_id=to, device_id_type=MESH)

    each(1, ys_n, lambda d: greet(device(z, x, core, (y + d) % ys_n)))
    greet(device(z, x, 1 - core, y))
    each(1, XS, lambda d: greet(device(z, (x + d) % XS, core, y)))
    each(1, zs_n, lambda d: greet(device((z + d) % zs_n, x, core, y)))

    summed = m_ref[...] + g_ref[...].astype(jnp.float32)
    left_part = dot(summed, q_ref[...])
    for k in range(ys_n):
        row, col = k // across, k % across
        part[k] = left_part[row * half : (row + 1) * half, col * lanes : (col + 1) * lanes]
    pl.semaphore_wait(barrier, (ys_n - 1) + 1 + (XS - 1) + (zs_n - 1))

    def y_of(d):
        return (y + d) % ys_n

    each(1, ys_n, lambda d: send(part.at[y_of(d)], ybuf.at[y], s_y.at[d], r_y.at[y], device(z, x, core, y_of(d))))
    ybuf[y] = part[y]
    each(1, ys_n, lambda d: came(ybuf.at[y_of(d)], r_y.at[y_of(d)]))
    total = ybuf[0]
    for k in range(1, ys_n):
        total = total + ybuf[k]
    chunks[y] = total
    each(1, ys_n, lambda d: send(chunks.at[y], chunks.at[y], s_y2.at[d], r_y2.at[y], device(z, x, core, y_of(d))))
    each(1, ys_n, lambda d: came(chunks.at[y_of(d)], r_y2.at[y_of(d)]))
    for k in range(ys_n):
        row, col = k // across, k % across
        a_ref[row * half : (row + 1) * half, col * lanes : (col + 1) * lanes] = chunks[k]

    left_raw = a_ref[...]
    wpart[0:zs_n] = dot(summed, left_raw, 0, 0).reshape(zs_n, XS, CORES, 8, -1)
    gpart[...] = dot(left_raw, left_raw, 0, 0).reshape(gpart.shape)
    wpart[zs_n] = gpart[y]

    def x_of(d):
        return (x + d) % XS

    def z_of(d):
        return (z + d) % zs_n

    partner = device(z, x, 1 - core, y)
    each(1, XS + 1, lambda d: send(
        wpart.at[:, x_of(d), 1 - core], cbuf.at[x_of(d)], s_c.at[d - 1], r_c.at[x_of(d)], partner))

    def forward(d):
        k = x_of(d)
        came(cbuf.at[k], r_c.at[k])
        xsum[k] = wpart[:, k, core] + cbuf[k]
        send(xsum.at[k], xbuf.at[x], s_x.at[d], r_x.at[x], device(z, k, core, y))

    each(1, XS, forward)
    came(cbuf.at[x], r_c.at[x])
    xbuf[x] = wpart[:, x, core] + cbuf[x]
    each(1, XS, lambda d: came(xbuf.at[x_of(d)], r_x.at[x_of(d)]))
    zsum[...] = (xbuf[0] + xbuf[1]) + (xbuf[2] + xbuf[3])
    each(1, zs_n, lambda d: send(zsum.at[zs_n], zgbuf.at[z], s_zg.at[d], r_zg.at[z], device(z_of(d), x, core, y)))
    each(1, zs_n, lambda d: send(zsum.at[z_of(d)], zbuf.at[z], s_z.at[d], r_z.at[z], device(z_of(d), x, core, y)))
    zgbuf[z] = zsum[zs_n]
    zbuf[z] = zsum[z]

    each(1, zs_n, lambda d: came(zgbuf.at[z_of(d)], r_zg.at[z_of(d)]))
    tile = zgbuf[0]
    for k in range(1, zs_n):
        tile = tile + zgbuf[k]
    gfull[y, x, core] = tile
    mine = gfull.at[y, x, core]
    each(1, ys_n, lambda d: send(mine, mine, s_gy.at[d], r_gy.at[y], device(z, x, core, y_of(d))))

    each(1, zs_n, lambda d: came(zbuf.at[z_of(d)], r_z.at[z_of(d)]))
    tile = zbuf[0]
    for k in range(1, zs_n):
        tile = tile + zbuf[k]
    wfull[z, x, core] = tile
    own = wfull.at[z, x, core]
    each(1, zs_n, lambda d: send(own, own, s_wz.at[d], r_wz.at[z], device(z_of(d), x, core, y)))

    each(1, ys_n, lambda d: came(gfull.at[y_of(d), x, core], r_gy.at[y_of(d)]))
    gx = gfull.at[:, x, core]
    each(1, XS, lambda d: send(gx, gx, s_gx.at[d], r_gx.at[x], device(z, x_of(d), core, y)))
    each(1, zs_n, lambda d: came(wfull.at[z_of(d), x, core], r_wz.at[z_of(d)]))
    wx = wfull.at[:, x, core]
    each(1, XS, lambda d: send(wx, wx, s_wx.at[d], r_wx.at[x], device(z, x_of(d), core, y)))

    each(1, XS, lambda d: came(gfull.at[:, x_of(d), core], r_gx.at[x_of(d)]))
    gc = gfull.at[:, :, core]
    send(gc, gc, s_gc, r_gc, partner)
    each(1, XS, lambda d: came(wfull.at[:, x_of(d), core], r_wx.at[x_of(d)]))
    wc = wfull.at[:, :, core]
    send(wc, wc, s_wc, r_wc, partner)
    came(gfull.at[:, :, 1 - core], r_gc)
    gram_ref[...] = gfull[...].reshape(gram_ref.shape)
    came(wfull.at[:, :, 1 - core], r_wc)
    w_ref[...] = wfull[...].reshape(w_ref.shape)

    def drain_y(d):
        sent(part.at[y_of(d)], s_y.at[d])
        sent(chunks.at[y], s_y2.at[d])
        sent(mine, s_gy.at[d])

    def drain_x(d):
        sent(xsum.at[x_of(d)], s_x.at[d])
        sent(gx, s_gx.at[d])
        sent(wx, s_wx.at[d])

    def drain_z(d):
        sent(zsum.at[zs_n], s_zg.at[d])
        sent(zsum.at[z_of(d)], s_z.at[d])
        sent(own, s_wz.at[d])

    each(1, ys_n, drain_y)
    each(1, XS, drain_x)
    each(1, zs_n, drain_z)
    each(1, XS + 1, lambda d: sent(wpart.at[:, x_of(d), 1 - core], s_c.at[d - 1]))
    sent(gc, s_gc)
    sent(wc, s_wc)


def reduce_all(zs_n, ys_n, momentum, gradient, right_basis):
    rows, cols = momentum.shape
    rank = right_basis.shape[1]
    f32 = jnp.float32
    lanes = 128
    half = rows * rank // (ys_n * lanes)
    sems = []
    for n in (ys_n, ys_n, XS, XS, zs_n, zs_n, ys_n, XS):
        sems += [pltpu.SemaphoreType.DMA((n,))] * 2
    sems += [pltpu.SemaphoreType.DMA] * 2
    for n in (zs_n, XS):
        sems += [pltpu.SemaphoreType.DMA((n,))] * 2
    sems += [pltpu.SemaphoreType.DMA] * 2
    vmem = pl.BlockSpec(memory_space=pltpu.VMEM)
    return pl.pallas_call(
        functools.partial(reduce_kernel, zs_n, ys_n),
        name="reduce_all",
        out_shape=(
            jax.ShapeDtypeStruct((rows, rank), f32),
            jax.ShapeDtypeStruct((cols, rank), f32),
            jax.ShapeDtypeStruct((rank, rank), f32),
        ),
        in_specs=[vmem] * 3,
        out_specs=(vmem,) * 3,
        scratch_shapes=[
            pltpu.VMEM((ys_n, half, lanes), f32),
            pltpu.VMEM((ys_n, half, lanes), f32),
            pltpu.VMEM((ys_n, half, lanes), f32),
            pltpu.VMEM((zs_n + 1, XS, CORES, 8, rank), f32),
            pltpu.VMEM((ys_n, XS, CORES, 8, rank), f32),
            pltpu.VMEM((XS, zs_n + 1, 8, rank), f32),
            pltpu.VMEM((XS, zs_n + 1, 8, rank), f32),
            pltpu.VMEM((XS, zs_n + 1, 8, rank), f32),
            pltpu.VMEM((zs_n + 1, 8, rank), f32),
            pltpu.VMEM((zs_n, 8, rank), f32),
            pltpu.VMEM((zs_n, 8, rank), f32),
            pltpu.VMEM((zs_n, XS, CORES, 8, rank), f32),
            pltpu.VMEM((ys_n, XS, CORES, 8, rank), f32),
            *sems,
        ],
        compiler_params=pltpu.CompilerParams(
            collective_id=0, has_side_effects=True, vmem_limit_bytes=VMEM_LIMIT
        ),
    )(momentum, gradient, right_basis)


BLOCK = 128


def factor_block(tiles):
    shape = (8, BLOCK)
    lane = lax.broadcasted_iota(jnp.int32, shape, 1)
    sub = lax.broadcasted_iota(jnp.int32, shape, 0)
    count = len(tiles)
    out = []

    def column(tile, k):
        return jnp.broadcast_to(tile[:, k : k + 1], shape)

    def row(tile, k):
        return jnp.broadcast_to(tile[k : k + 1, :], shape)

    tiles = list(tiles)
    for t in range(count):
        base = 8 * t
        here = (lane >= base) & (lane < base + 8)
        tile = tiles[t]
        cols = [column(tile, base + c) for c in range(8)]
        start = jnp.where(here, jnp.where(lane - base == sub, 1.0, 0.0), tile)
        scale, rows, low = [], [], {}
        for p in range(8):
            r = lax.rsqrt(row(cols[p], p))
            lp = cols[p] * r
            for c in range(p + 1, 8):
                low[p, c] = row(lp, c)
                cols[c] = cols[c] - lp * low[p, c]
            w = row(start, p)
            for q in range(p):
                w = w - low[q, p] * rows[q]
            rows.append(w * r)
            scale.append(r)
        done = rows[7]
        for p in range(7):
            done = jnp.where(sub == p, rows[p], done)
        out.append(jnp.where(lane < base + 8, done, 0.0))
        if t + 1 == count:
            break
        solved = [None] * 8
        for p in reversed(range(8)):
            w = rows[p]
            for q in range(p + 1, 8):
                w = w - low[p, q] * solved[q]
            solved[p] = w * scale[p]
        for i in range(t + 1, count):
            acc = jnp.where(here, 0.0, tiles[i])
            for p in range(8):
                acc = acc - column(tiles[i], base + p) * solved[p]
            tiles[i] = acc
    return out


def factor_kernel(gram_ref, inv_ref, work, diag):
    size = gram_ref.shape[0]
    work[...] = gram_ref[...]
    inv_ref[...] = jnp.zeros_like(inv_ref)
    lane = lax.broadcasted_iota(jnp.int32, (BLOCK, size), 1)

    @pl.loop(0, size // BLOCK)
    def _(b):
        off = pl.multiple_of(b * BLOCK, BLOCK)
        here = pl.ds(off, BLOCK)
        tiles = [work[pl.ds(pl.multiple_of(off + 8 * i, 8), 8), here] for i in range(BLOCK // 8)]
        for i, tile in enumerate(factor_block(tiles)):
            diag[8 * i : 8 * i + 8, :] = tile
        top = diag[...]
        inv_ref[here, :] = dot(top, inv_ref[here, :])
        inv_ref[here, here] = top

        @pl.when(b + 1 < size // BLOCK)
        def _():
            panel = jnp.where(lane >= off + BLOCK, dot(top, work[here, :]), 0.0)[:, BLOCK:]
            work[BLOCK:, BLOCK:] = work[BLOCK:, BLOCK:] - dot(panel, panel, 0, 0)
            inv_ref[BLOCK:, :] = inv_ref[BLOCK:, :] - dot(panel, inv_ref[here, :], 0, 0)


def factor(gram):
    vmem = pl.BlockSpec(memory_space=pltpu.VMEM)
    return pl.pallas_call(
        factor_kernel,
        name="factor",
        out_shape=jax.ShapeDtypeStruct(gram.shape, jnp.float32),
        in_specs=[vmem],
        out_specs=vmem,
        scratch_shapes=[pltpu.VMEM(gram.shape, jnp.float32), pltpu.VMEM((BLOCK, BLOCK), jnp.float32)],
        compiler_params=pltpu.CompilerParams(vmem_limit_bytes=VMEM_LIMIT),
    )(gram)


def finish_kernel(
    ys_n, total_rows, factor_value, m_ref, g_ref, a_ref, w_ref, inv_ref,
    update_ref, momentum_ref, left_ref, basis_ref, right, norms, s_n, r_n,
):
    z, x, core, y = place()
    barrier = pltpu.get_barrier_semaphore()

    def peer(d):
        return device(z, x, core, (y + d) % ys_n)

    each(1, ys_n, lambda d: pl.semaphore_signal(barrier, inc=1, device_id=peer(d), device_id_type=MESH))
    inverse = inv_ref[...]
    right[...] = dot(w_ref[...], inverse, 1, 1)
    values = right[...]
    norms[y] = jnp.sum(values * values, axis=0, keepdims=True)
    pl.semaphore_wait(barrier, ys_n - 1)

    def copy(d, slot):
        return pltpu.make_async_remote_copy(
            src_ref=norms.at[slot], dst_ref=norms.at[slot], send_sem=s_n.at[d], recv_sem=r_n.at[slot],
            device_id=peer(d), device_id_type=MESH,
        )

    each(1, ys_n, lambda d: copy(d, y).start())
    left = dot(a_ref[...], inverse, 1, 1)
    left_ref[...] = left * math.sqrt(total_rows)
    summed = m_ref[...] + g_ref[...].astype(jnp.float32)
    momentum_ref[...] = summed - 0.5 * dot(left, values, 1, 1)
    each(1, ys_n, lambda d: copy(d, (y + d) % ys_n).wait_recv())
    total = norms[0]
    for k in range(1, ys_n):
        total = total + norms[k]
    column_norm = jnp.sqrt(total + EPSILON)
    scaled = left * (factor_value / column_norm)
    update_ref[...] = dot(scaled, values, 1, 1).astype(update_ref.dtype)
    me = pl.multiple_of(lax.axis_index("fsdp") * 8, 8)
    basis_ref[...] = right[pl.ds(me, 8), :] / column_norm
    each(1, ys_n, lambda d: copy(d, y).wait_send())


def finish(ys_n, total_rows, factor_value, momentum, gradient, left_raw, w, inverse):
    rows, cols = momentum.shape
    rank = w.shape[1]
    f32 = jnp.float32
    vmem = pl.BlockSpec(memory_space=pltpu.VMEM)
    return pl.pallas_call(
        functools.partial(finish_kernel, ys_n, total_rows, factor_value),
        name="finish",
        out_shape=(
            jax.ShapeDtypeStruct((rows, cols), jnp.bfloat16),
            jax.ShapeDtypeStruct((rows, cols), f32),
            jax.ShapeDtypeStruct((rows, rank), f32),
            jax.ShapeDtypeStruct((8, rank), f32),
        ),
        in_specs=[vmem] * 5,
        out_specs=(vmem,) * 4,
        scratch_shapes=[
            pltpu.VMEM((cols, rank), f32),
            pltpu.VMEM((ys_n, 1, rank), f32),
            pltpu.SemaphoreType.DMA((ys_n,)),
            pltpu.SemaphoreType.DMA((ys_n,)),
        ],
        compiler_params=pltpu.CompilerParams(
            collective_id=1, has_side_effects=True, vmem_limit_bytes=VMEM_LIMIT
        ),
    )(momentum, gradient, left_raw, w, inverse)


def on_device(momentum, gradient, right_basis):
    groups = lax.axis_size("fsdp")
    ys_n = lax.axis_size("tensor")
    zs_n = groups // (XS * CORES)
    left_raw, w, gram = reduce_all(zs_n, ys_n, momentum, gradient, right_basis)
    inverse = factor(gram)
    total_rows = momentum.shape[0] * groups
    total_cols = momentum.shape[1] * ys_n
    ratio = math.sqrt(total_rows / total_cols)
    return finish(ys_n, total_rows, ratio, momentum, gradient, left_raw, w, inverse)


def solution(mesh):
    in_specs = (P("fsdp", "tensor"), P("fsdp", "tensor"), P("tensor", None))
    out_specs = (
        P("fsdp", "tensor"),
        P("fsdp", "tensor"),
        P("fsdp", None),
        P(("tensor", "fsdp"), None),
    )
    return jax.shard_map(
        on_device, mesh=mesh, in_specs=in_specs, out_specs=out_specs, check_vma=False
    )
```

time: 905 us -> 153 us (0.17)
  waiting for transfers between devices: 697 us -> 0 us
  Pallas kernels: 0 us -> 147 us
  other arithmetic: 125 us -> 0 us
  matrix products: 27.3 us -> 0 us
  between operations: 16.8 us -> 0.67 us
  local copies, waits for them, and re-layouts: 19.2 us -> 5.22 us
  blocking collectives: 13.5 us -> 0 us
    psum x2 -> x0, waiting for transfers between devices: 370 us -> none  [the longest x1 282 us: on_device(): gram = lax.psum(jnp.dot(left_raw.T, left_raw, precision=highest), 'fsdp')]
    reduce_scatter x1 -> x0, waiting for transfers between devices: 202 us -> none  [on_device(): lax.psum_scatter(jnp.dot(summed.T, left, precision=highest), 'fsdp', scat...]
    pallas_call x0 -> x3, Pallas kernels: none -> 147 us  [the longest x1 101 us: reduce_all(): pl.pallas_call(functools.partial(reduce_kernel, zs_n, ys_n), name='reduce...]
    all_gather x1 -> x0, waiting for transfers between devices: 125 us -> none  [on_device(): right_full = lax.all_gather(right_rows, 'fsdp', axis=0, tiled=True)]
    another operation x17 -> x0, other arithmetic: 121 us -> none  [the longest x14 78.6 us: on_device(): factor_lower = jnp.linalg.cholesky(gram)]
    dot_general x5 -> x0, matrix products: 15.3 us -> none  [the longest x1 3.64 us: planes_for(): product = jnp.dot(left, right_rows.T, precision=highest)]
    another operation x17 -> x0, local copies, waits for them, and re-layouts: 14.1 us -> none
    psum x1 -> x0, blocking collectives: 13.5 us -> none  [block_norms(): squares = lax.psum(jnp.sum(right_full * right_full, axis=0), 'tensor')]
  transfers between devices with their start and end apart: 4 -> 0, of which waited for: 4 -> 0; matrix products, arithmetic and copies ran while one was open for 0% -> 0% of each run, Pallas kernels for 0% -> 0%
where the time goes in v1:
time: 153 us
  Pallas kernels  147 us (96%)
  local copies, waits for them, and re-layouts  5.22 us (3%)
    pallas_call x1, Pallas kernels, reduce_all(): pl.pallas_call(functools.partial(reduce_kernel, zs_n, ys_n), name='reduce...  101 us
    pallas_call x1, Pallas kernels, factor(): pl.pallas_call(factor_kernel, name='factor', out_shape=jax.ShapeDtypeStru...  30 us
    pallas_call x1, Pallas kernels, finish(): pl.pallas_call(functools.partial(finish_kernel, ys_n, total_rows, factor_...  16 us
    unnamed x8, local copies, waits for them, and re-layouts  5.22 us

profile of v1, /device:TPU:1, one launch (start us, length us, event | category | flops | bytes accessed | tf_op | source)
XLA Modules:
  0.0 152.9 jit_solution(13093927688827969991)
XLA Ops:
  0.6 101.1 %reduce_all.1 = (f32[240,512]{1,0:T(8,128)}, f32[768,512]{1,0:T(8,128)}, f32[512,512]{1,0:T(8,128)}) custom-call(f32[240,768]{1,0:T(8,128)} %m_ref.3, bf16[240,768]{1,0:T(8,128)(2,1)} %g_ref.3, f32[768,512]{1,0:T(8,128)} %q_ref.1), custom_call_target="tpu_custom_call" | custom-call | tf_op jit(solution)/shard_map/reduce_all/pallas_call | solution.py:199
  101.7 30.0 %factor.1.inv_ref = f32[512,512]{1,0:T(8,128)} custom-call(f32[512,512]{1,0:T(8,128)} %get-tuple-element.9.gram_ref), custom_call_target="tpu_custom_call" | custom-call | tf_op jit(solution)/shard_map/factor/pallas_call | solution.py:312
  131.7 16.0 %finish.1 = (bf16[240,768]{1,0:T(8,128)(2,1)}, f32[240,768]{1,0:T(8,128)}, f32[240,512]{1,0:T(8,128)}, f32[8,512]{1,0:T(8,128)}) custom-call(f32[240,768]{1,0:T(8,128)} %m_ref.3, bf16[240,768]{1,0:T(8,128)(2,1)} %g_ref.3, f32[240,512]{1,0:T(8,128)} %get-tuple-element.7.a_ref, f32[768,512]{1,0:T(8,128)} %get-tuple-element.8.w_ref, f32[512,512]{1,0:T(8,128)} %factor.1.inv_ref), custom_call_target="tpu_custom_call" | custom-call | tf_op jit(solution)/shard_map/finish/pallas_call | solution.py:368
  147.6 0.0 copy-start
  147.7 0.0 copy-start.1
  147.7 1.8 %copy.11 = bf16[240,768]{1,0:T(8,128)(2,1)} copy(bf16[240,768]{1,0:T(8,128)(2,1)} %get-tuple-element.14) | data formatting | bytes 737280
  149.5 2.0 %copy.12 = f32[240,768]{1,0:T(8,128)} copy(f32[240,768]{1,0:T(8,128)} %get-tuple-element.15) | data formatting | bytes 1474560
  151.5 0.0 copy-done
  151.5 0.8 copy.13
  152.3 0.0 copy-done.1
  152.3 0.6 copy.14
Async XLA Ops:
  147.6 3.9 %copy-start = (f32[240,512]{1,0:T(8,128)S(1)}, f32[240,512]{1,0:T(8,128)}, u32[]{:S(2)}) copy-start(f32[240,512]{1,0:T(8,128)} %get-tuple-element.16) | copy-start | bytes 1474564
  147.7 4.6 %copy-start.1 = (f32[8,512]{1,0:T(8,128)S(1)}, f32[8,512]{1,0:T(8,128)}, u32[]{:S(2)}) copy-start(f32[8,512]{1,0:T(8,128)} %get-tuple-element.17) | copy-start | bytes 49156

commit v2 on v0

v2 whole, which is shorter than its diff:
```python
import functools
import math

import jax
import jax.numpy as jnp
from jax import lax
from jax.experimental import pallas as pl
from jax.experimental.pallas import tpu as pltpu
from jax.sharding import PartitionSpec as P

EPSILON = 1e-06
HIGHEST = lax.Precision.HIGHEST
MESH = pl.DeviceIdType.MESH
XS, CORES = 4, 2
VMEM_LIMIT = 60 * 1024 * 1024


def dot(a, b, lhs=1, rhs=0):
    return lax.dot_general(
        a, b, (((lhs,), (rhs,)), ((), ())), precision=HIGHEST, preferred_element_type=jnp.float32
    )


def split(a):
    high = a.astype(jnp.bfloat16)
    return high, (a - high.astype(jnp.float32)).astype(jnp.bfloat16)


def dot3(a, b, lhs=1, rhs=0):
    def one(p, q):
        return lax.dot_general(p, q, (((lhs,), (rhs,)), ((), ())), preferred_element_type=jnp.float32)

    return one(a[0], b[0]) + (one(a[0], b[1]) + one(a[1], b[0]))


def place():
    f = lax.axis_index("fsdp")
    y = lax.axis_index("tensor")
    return f // (XS * CORES), (f // CORES) % XS, f % CORES, y


def device(z, x, core, y):
    return ((z * XS + x) * CORES + core, y)


def each(start, stop, body):
    def step(i, carry):
        body(i)
        return carry

    lax.fori_loop(start, stop, step, 0)


BLOCK = 128


def factor_block(tiles):
    shape = (8, BLOCK)
    lane = lax.broadcasted_iota(jnp.int32, shape, 1)
    sub = lax.broadcasted_iota(jnp.int32, shape, 0)
    count = len(tiles)
    out = []

    def column(tile, k):
        return jnp.broadcast_to(tile[:, k : k + 1], shape)

    def row(tile, k):
        return jnp.broadcast_to(tile[k : k + 1, :], shape)

    tiles = list(tiles)
    for t in range(count):
        base = 8 * t
        here = (lane >= base) & (lane < base + 8)
        tile = tiles[t]
        cols = [column(tile, base + c) for c in range(8)]
        start = jnp.where(here, jnp.where(lane - base == sub, 1.0, 0.0), tile)
        scale, rows, low = [], [], {}
        for p in range(8):
            r = lax.rsqrt(row(cols[p], p))
            lp = cols[p] * r
            for c in range(p + 1, 8):
                low[p, c] = row(lp, c)
                cols[c] = cols[c] - lp * low[p, c]
            w = row(start, p)
            for q in range(p):
                w = w - low[q, p] * rows[q]
            rows.append(w * r)
            scale.append(r)
        done = rows[7]
        for p in range(7):
            done = jnp.where(sub == p, rows[p], done)
        out.append(jnp.where(lane < base + 8, done, 0.0))
        if t + 1 == count:
            break
        solved = [None] * 8
        for p in reversed(range(8)):
            w = rows[p]
            for q in range(p + 1, 8):
                w = w - low[p, q] * solved[q]
            solved[p] = w * scale[p]
        for i in range(t + 1, count):
            acc = jnp.where(here, 0.0, tiles[i])
            for p in range(8):
                acc = acc - column(tiles[i], base + p) * solved[p]
            tiles[i] = acc
    return out


def factor_step(b, work, top_ref, between):
    size = work.shape[0]
    off = pl.multiple_of(b * BLOCK, BLOCK)
    here = pl.ds(off, BLOCK)
    tiles = [work[pl.ds(pl.multiple_of(off + 8 * i, 8), 8), here] for i in range(BLOCK // 8)]
    for i, tile in enumerate(factor_block(tiles)):
        top_ref[8 * i : 8 * i + 8, :] = tile
    between()
    lane = lax.broadcasted_iota(jnp.int32, (BLOCK, size), 1)
    top = top_ref[...]
    panel = dot(top, work[here, :])
    work[here, :] = jnp.where(lane < off, panel, 0.0)
    work[here, here] = top

    @pl.when(b + 1 < size // BLOCK)
    def _():
        after = jnp.where(lane >= off + BLOCK, panel, 0.0)
        shape = (size - BLOCK, size)
        below = lax.broadcasted_iota(jnp.int32, shape, 0) >= off
        lanes = lax.broadcasted_iota(jnp.int32, shape, 1)
        gone = below & (lanes >= off) & (lanes < off + BLOCK)
        row = work[here, :] + after
        work[BLOCK:, :] = jnp.where(gone, 0.0, work[BLOCK:, :]) - dot(after[:, BLOCK:], row, 0, 0)


def kernel(
    zs_n, ys_n, total_rows, ratio, m_ref, g_ref, q_ref, update_ref, momentum_ref, left_ref, basis_ref,
    part, ybuf, chunks, raw, gpart, gcbuf, gxsum, gxbuf, gzsum, gzbuf, gfull,
    wpart, wcbuf, wxsum, wxbuf, wzsum, wzbuf, wfull, work, top, right, norms,
    s_y, r_y, s_y2, r_y2, s_n, r_n,
    s_hc, r_hc, s_hx, r_hx, s_hz, r_hz, s_gy, r_gy, s_gx, r_gx, s_gc, r_gc,
    s_c, r_c, s_x, r_x, s_z, r_z, s_wz, r_wz, s_wx, r_wx, s_wc, r_wc,
):
    z, x, core, y = place()
    half = part.shape[1]
    lanes = part.shape[2]
    across = raw.shape[1] // lanes

    def send(src, dst, ssem, rsem, to):
        pltpu.make_async_remote_copy(
            src_ref=src, dst_ref=dst, send_sem=ssem, recv_sem=rsem, device_id=to, device_id_type=MESH
        ).start()

    def done(ref, sem):
        pltpu.make_async_copy(ref, ref, sem).wait()

    def total(ref):
        acc = ref[0]
        for k in range(1, ref.shape[0]):
            acc = acc + ref[k]
        return acc

    def x_of(d):
        return (x + d) % XS

    def y_of(d):
        return (y + d) % ys_n

    def z_of(d):
        return (z + d) % zs_n

    def at_x(k):
        return device(z, k, core, y)

    def at_y(k):
        return device(z, x, core, k)

    def at_z(k):
        return device(k, x, core, y)

    partner = device(z, x, 1 - core, y)
    barrier = pltpu.get_barrier_semaphore()

    def greet(to):
        pl.semaphore_signal(barrier, inc=1, device_id=to, device_id_type=MESH)

    each(1, ys_n, lambda d: greet(at_y(y_of(d))))
    greet(partner)
    each(1, XS, lambda d: greet(at_x(x_of(d))))
    each(1, zs_n, lambda d: greet(at_z(z_of(d))))

    summed = split(m_ref[...] + g_ref[...].astype(jnp.float32))
    left_part = dot3(summed, split(q_ref[...]))
    for k in range(ys_n):
        row, col = k // across, k % across
        part[k] = left_part[row * half : (row + 1) * half, col * lanes : (col + 1) * lanes]
    pl.semaphore_wait(barrier, (ys_n - 1) + 1 + (XS - 1) + (zs_n - 1))

    each(1, ys_n, lambda d: send(part.at[y_of(d)], ybuf.at[y], s_y.at[d], r_y.at[y], at_y(y_of(d))))
    ybuf[y] = part[y]
    each(1, ys_n, lambda d: done(ybuf.at[y_of(d)], r_y.at[y_of(d)]))
    chunks[y] = total(ybuf)
    each(1, ys_n, lambda d: send(chunks.at[y], chunks.at[y], s_y2.at[d], r_y2.at[y], at_y(y_of(d))))
    each(1, ys_n, lambda d: done(chunks.at[y_of(d)], r_y2.at[y_of(d)]))
    for k in range(ys_n):
        row, col = k // across, k % across
        raw[row * half : (row + 1) * half, col * lanes : (col + 1) * lanes] = chunks[k]

    per = gpart.shape[0]
    pair = raw[:, pl.ds(pl.multiple_of((y // per) * 128, 128), 128)]
    gpart[...] = dot(pair, raw[...], 0, 0).reshape(gpart.shape)
    plane = y % per
    ghalf = gpart.at[plane, :, 1 - core]
    send(ghalf, gcbuf, s_hc, r_hc, partner)

    wpart[...] = dot3(summed, split(raw[...]), 0, 0).reshape(wpart.shape)
    each(1, XS + 1, lambda d: send(
        wpart.at[:, x_of(d), 1 - core], wcbuf.at[x_of(d)], s_c.at[d - 1], r_c.at[x_of(d)], partner))

    done(gcbuf, r_hc)
    gxsum[...] = gpart[plane, :, core] + gcbuf[...]
    each(1, XS, lambda d: send(gxsum.at[x_of(d)], gxbuf.at[x], s_hx.at[d], r_hx.at[x], at_x(x_of(d))))
    gxbuf[x] = gxsum[x]

    def w_forward(d):
        k = x_of(d)
        done(wcbuf.at[k], r_c.at[k])
        wxsum[k] = wpart[:, k, core] + wcbuf[k]
        send(wxsum.at[k], wxbuf.at[x], s_x.at[d], r_x.at[x], at_x(k))

    each(1, XS, w_forward)
    each(1, XS, lambda d: done(gxbuf.at[x_of(d)], r_hx.at[x_of(d)]))
    gzsum[...] = total(gxbuf)
    each(1, zs_n, lambda d: send(gzsum, gzbuf.at[z], s_hz.at[d], r_hz.at[z], at_z(z_of(d))))
    gzbuf[z] = gzsum[...]
    done(wcbuf.at[x], r_c.at[x])
    wxbuf[x] = wpart[:, x, core] + wcbuf[x]

    each(1, zs_n, lambda d: done(gzbuf.at[z_of(d)], r_hz.at[z_of(d)]))
    gfull[y, x, core] = total(gzbuf)
    gown = gfull.at[y, x, core]
    each(1, ys_n, lambda d: send(gown, gown, s_gy.at[d], r_gy.at[y], at_y(y_of(d))))

    each(1, XS, lambda d: done(wxbuf.at[x_of(d)], r_x.at[x_of(d)]))
    wzsum[...] = total(wxbuf)
    each(1, zs_n, lambda d: send(wzsum.at[z_of(d)], wzbuf.at[z], s_z.at[d], r_z.at[z], at_z(z_of(d))))
    wzbuf[z] = wzsum[z]

    each(1, ys_n, lambda d: done(gfull.at[y_of(d), x, core], r_gy.at[y_of(d)]))
    gx = gfull.at[:, x, core]
    each(1, XS, lambda d: send(gx, gx, s_gx.at[d], r_gx.at[x], at_x(x_of(d))))
    each(1, XS, lambda d: done(gfull.at[:, x_of(d), core], r_gx.at[x_of(d)]))
    gc = gfull.at[:, :, core]
    send(gc, gc, s_gc, r_gc, partner)
    done(gfull.at[:, :, 1 - core], r_gc)
    work[...] = gfull[...].reshape(work.shape)

    each(1, zs_n, lambda d: done(wzbuf.at[z_of(d)], r_z.at[z_of(d)]))
    wfull[z, x, core] = total(wzbuf)
    wown = wfull.at[z, x, core]
    each(1, zs_n, lambda d: send(wown, wown, s_wz.at[d], r_wz.at[z], at_z(z_of(d))))
    wx = wfull.at[:, x, core]
    wc = wfull.at[:, :, core]

    @pl.loop(0, work.shape[0] // BLOCK)
    def _(b):
        def between():
            @pl.when(b == 0)
            def _():
                each(1, zs_n, lambda d: done(wfull.at[z_of(d), x, core], r_wz.at[z_of(d)]))
                each(1, XS, lambda d: send(wx, wx, s_wx.at[d], r_wx.at[x], at_x(x_of(d))))

            @pl.when(b == 2)
            def _():
                each(1, XS, lambda d: done(wfull.at[:, x_of(d), core], r_wx.at[x_of(d)]))
                send(wc, wc, s_wc, r_wc, partner)

        factor_step(b, work, top, between)

    done(wfull.at[:, :, 1 - core], r_wc)

    inverse = split(work[...])
    right[...] = dot3(split(wfull[...].reshape(right.shape)), inverse, 1, 1)
    values = right[...]
    norms[y] = jnp.sum(values * values, axis=0, keepdims=True)
    each(1, ys_n, lambda d: send(norms.at[y], norms.at[y], s_n.at[d], r_n.at[y], at_y(y_of(d))))
    rows = split(values)
    left = dot3(split(raw[...]), inverse, 1, 1)
    left_ref[...] = left * math.sqrt(total_rows)
    product = dot3(split(left), rows, 1, 1)
    momentum_ref[...] = (m_ref[...] + g_ref[...].astype(jnp.float32)) - 0.5 * product
    each(1, ys_n, lambda d: done(norms.at[y_of(d)], r_n.at[y_of(d)]))
    column_norm = jnp.sqrt(total(norms) + EPSILON)
    update_ref[...] = dot3(split(left * (ratio / column_norm)), rows, 1, 1).astype(update_ref.dtype)
    me = pl.multiple_of(lax.axis_index("fsdp") * 8, 8)
    basis_ref[...] = right[pl.ds(me, 8), :] / column_norm

    def sent_y(d):
        done(part.at[y_of(d)], s_y.at[d])
        done(chunks.at[y], s_y2.at[d])
        done(gown, s_gy.at[d])
        done(norms.at[y], s_n.at[d])

    def sent_x(d):
        done(gxsum.at[x_of(d)], s_hx.at[d])
        done(gx, s_gx.at[d])
        done(wxsum.at[x_of(d)], s_x.at[d])
        done(wx, s_wx.at[d])

    def sent_z(d):
        done(gzsum, s_hz.at[d])
        done(wzsum.at[z_of(d)], s_z.at[d])
        done(wown, s_wz.at[d])

    each(1, ys_n, sent_y)
    each(1, XS, sent_x)
    each(1, zs_n, sent_z)
    each(1, XS + 1, lambda d: done(wpart.at[:, x_of(d), 1 - core], s_c.at[d - 1]))
    done(ghalf, s_hc)
    done(gc, s_gc)
    done(wc, s_wc)


def on_device(momentum, gradient, right_basis):
    rows, cols = momentum.shape
    rank = right_basis.shape[1]
    groups = lax.axis_size("fsdp")
    ys_n = lax.axis_size("tensor")
    zs_n = groups // (XS * CORES)
    total_rows = rows * groups
    ratio = math.sqrt(total_rows / (cols * ys_n))
    f32 = jnp.float32
    lanes = 128
    half = rows * rank // (ys_n * lanes)
    per = lanes * ys_n // rank

    def buffer(*shape):
        return pltpu.VMEM(shape, f32)

    one = [pltpu.SemaphoreType.DMA] * 2

    def sems(n):
        return [pltpu.SemaphoreType.DMA((n,))] * 2

    gsum = buffer(XS, 8, rank)
    wsum = buffer(XS, zs_n, 8, rank)
    vmem = pl.BlockSpec(memory_space=pltpu.VMEM)
    return pl.pallas_call(
        functools.partial(kernel, zs_n, ys_n, total_rows, ratio),
        name="step",
        out_shape=(
            jax.ShapeDtypeStruct((rows, cols), jnp.bfloat16),
            jax.ShapeDtypeStruct((rows, cols), f32),
            jax.ShapeDtypeStruct((rows, rank), f32),
            jax.ShapeDtypeStruct((8, rank), f32),
        ),
        in_specs=[vmem] * 3,
        out_specs=(vmem,) * 4,
        scratch_shapes=[
            buffer(ys_n, half, lanes), buffer(ys_n, half, lanes), buffer(ys_n, half, lanes), buffer(rows, rank),
            buffer(per, XS, CORES, 8, rank), gsum, gsum, gsum, buffer(8, rank), buffer(zs_n, 8, rank),
            buffer(ys_n, XS, CORES, 8, rank),
            buffer(zs_n, XS, CORES, 8, rank), wsum, wsum, wsum, buffer(zs_n, 8, rank), buffer(zs_n, 8, rank),
            buffer(zs_n, XS, CORES, 8, rank),
            buffer(rank, rank), buffer(BLOCK, BLOCK), buffer(cols, rank), buffer(ys_n, 1, rank),
            *sems(ys_n), *sems(ys_n), *sems(ys_n),
            *one, *sems(XS), *sems(zs_n), *sems(ys_n), *sems(XS), *one,
            *sems(XS), *sems(XS), *sems(zs_n), *sems(zs_n), *sems(XS), *one,
        ],
        compiler_params=pltpu.CompilerParams(
            collective_id=0, has_side_effects=True, vmem_limit_bytes=VMEM_LIMIT
        ),
    )(momentum, gradient, right_basis)


def solution(mesh):
    in_specs = (P("fsdp", "tensor"), P("fsdp", "tensor"), P("tensor", None))
    out_specs = (
        P("fsdp", "tensor"),
        P("fsdp", "tensor"),
        P("fsdp", None),
        P(("tensor", "fsdp"), None),
    )
    return jax.shard_map(
        on_device, mesh=mesh, in_specs=in_specs, out_specs=out_specs, check_vma=False
    )
```

time: 905 us -> 121 us (0.13)
  waiting for transfers between devices: 697 us -> 0 us
  other arithmetic: 125 us -> 0 us
  Pallas kernels: 0 us -> 115 us
  matrix products: 27.3 us -> 0 us
  between operations: 16.8 us -> 0.66 us
  local copies, waits for them, and re-layouts: 19.2 us -> 5.22 us
  blocking collectives: 13.5 us -> 0 us
    psum x2 -> x0, waiting for transfers between devices: 370 us -> none  [the longest x1 282 us: on_device(): gram = lax.psum(jnp.dot(left_raw.T, left_raw, precision=highest), 'fsdp')]
    reduce_scatter x1 -> x0, waiting for transfers between devices: 202 us -> none  [on_device(): lax.psum_scatter(jnp.dot(summed.T, left, precision=highest), 'fsdp', scat...]
    all_gather x1 -> x0, waiting for transfers between devices: 125 us -> none  [on_device(): right_full = lax.all_gather(right_rows, 'fsdp', axis=0, tiled=True)]
    another operation x17 -> x0, other arithmetic: 121 us -> none  [the longest x14 78.6 us: on_device(): factor_lower = jnp.linalg.cholesky(gram)]
    pallas_call x0 -> x1, Pallas kernels: none -> 115 us  [on_device(): pl.pallas_call(functools.partial(kernel, zs_n, ys_n, total_rows, ratio),...]
    dot_general x5 -> x0, matrix products: 15.3 us -> none  [the longest x1 3.64 us: planes_for(): product = jnp.dot(left, right_rows.T, precision=highest)]
    another operation x17 -> x0, local copies, waits for them, and re-layouts: 14.1 us -> none
    psum x1 -> x0, blocking collectives: 13.5 us -> none  [block_norms(): squares = lax.psum(jnp.sum(right_full * right_full, axis=0), 'tensor')]
  transfers between devices with their start and end apart: 4 -> 0, of which waited for: 4 -> 0; matrix products, arithmetic and copies ran while one was open for 0% -> 0% of each run, Pallas kernels for 0% -> 0%
where the time goes in v2:
time: 121 us; the launch traced here: 120 us
  Pallas kernels  115 us (95%)
  local copies, waits for them, and re-layouts  5.22 us (4%)
    pallas_call x1, Pallas kernels, on_device(): pl.pallas_call(functools.partial(kernel, zs_n, ys_n, total_rows, ratio),...  115 us
    unnamed x8, local copies, waits for them, and re-layouts  5.22 us

profile of v2, /device:TPU:1, one launch (start us, length us, event | category | flops | bytes accessed | tf_op | source)
XLA Modules:
  0.0 120.4 jit_solution(10291225790182248960)
XLA Ops:
  0.6 114.5 %step.1 = (bf16[240,768]{1,0:T(8,128)(2,1)}, f32[240,768]{1,0:T(8,128)}, f32[240,512]{1,0:T(8,128)}, f32[8,512]{1,0:T(8,128)}) custom-call(f32[240,768]{1,0:T(8,128)} %m_ref.1, bf16[240,768]{1,0:T(8,128)(2,1)} %g_ref.1, f32[768,512]{1,0:T(8,128)} %q_ref.1), custom_call_target="tpu_custom_call" | custom-call | tf_op jit(solution)/shard_map/step/pallas_call | solution.py:346
  115.1 0.0 copy-start
  115.2 0.0 copy-start.1
  115.2 1.8 %copy.11 = bf16[240,768]{1,0:T(8,128)(2,1)} copy(bf16[240,768]{1,0:T(8,128)(2,1)} %get-tuple-element.8) | data formatting | bytes 737280
  117.0 2.0 %copy.12 = f32[240,768]{1,0:T(8,128)} copy(f32[240,768]{1,0:T(8,128)} %get-tuple-element.9) | data formatting | bytes 1474560
  119.0 0.0 copy-done
  119.0 0.8 copy.13
  119.8 0.0 copy-done.1
  119.8 0.6 copy.14
Async XLA Ops:
  115.1 3.9 %copy-start = (f32[240,512]{1,0:T(8,128)S(1)}, f32[240,512]{1,0:T(8,128)}, u32[]{:S(2)}) copy-start(f32[240,512]{1,0:T(8,128)} %get-tuple-element.10) | copy-start | bytes 1474564
  115.2 4.6 %copy-start.1 = (f32[8,512]{1,0:T(8,128)S(1)}, f32[8,512]{1,0:T(8,128)}, u32[]{:S(2)}) copy-start(f32[8,512]{1,0:T(8,128)} %get-tuple-element.11) | copy-start | bytes 49156

commit v3 on v2

--- a/solution.py
+++ b/solution.py
@@ -12,7 +12,7 @@
 HIGHEST = lax.Precision.HIGHEST
 MESH = pl.DeviceIdType.MESH
 XS, CORES = 4, 2
-VMEM_LIMIT = 60 * 1024 * 1024
+VMEM_LIMIT = 24 * 1024 * 1024
 
 
 def dot(a, b, lhs=1, rhs=0):
@@ -49,6 +49,14 @@
         return carry
 
     lax.fori_loop(start, stop, step, 0)
+
+
+def each_peer(count, body):
+    def step(k):
+        off = (k + 1) // 2
+        body(count // 2 + off * (1 - 2 * (k % 2)))
+
+    each(0, count - 1, step)
 
 
 BLOCK = 128
@@ -76,7 +84,7 @@
         start = jnp.where(here, jnp.where(lane - base == sub, 1.0, 0.0), tile)
         scale, rows, low = [], [], {}
         for p in range(8):
-            r = lax.rsqrt(row(cols[p], p))
+            r = row(lax.rsqrt(cols[p]), p)
             lp = cols[p] * r
             for c in range(p + 1, 8):
                 low[p, c] = row(lp, c)
@@ -95,12 +103,12 @@
         solved = [None] * 8
         for p in reversed(range(8)):
             w = rows[p]
-            for q in range(p + 1, 8):
+            for q in reversed(range(p + 1, 8)):
                 w = w - low[p, q] * solved[q]
             solved[p] = w * scale[p]
         for i in range(t + 1, count):
             acc = jnp.where(here, 0.0, tiles[i])
-            for p in range(8):
+            for p in reversed(range(8)):
                 acc = acc - column(tiles[i], base + p) * solved[p]
             tiles[i] = acc
     return out
@@ -116,7 +124,8 @@
     between()
     lane = lax.broadcasted_iota(jnp.int32, (BLOCK, size), 1)
     top = top_ref[...]
-    panel = dot(top, work[here, :])
+    inverse = split(top)
+    panel = dot3(inverse, split(work[here, :]))
     work[here, :] = jnp.where(lane < off, panel, 0.0)
     work[here, here] = top
 
@@ -128,12 +137,12 @@
         lanes = lax.broadcasted_iota(jnp.int32, shape, 1)
         gone = below & (lanes >= off) & (lanes < off + BLOCK)
         row = work[here, :] + after
-        work[BLOCK:, :] = jnp.where(gone, 0.0, work[BLOCK:, :]) - dot(after[:, BLOCK:], row, 0, 0)
+        work[BLOCK:, :] = jnp.where(gone, 0.0, work[BLOCK:, :]) - dot3(split(after[:, BLOCK:]), split(row), 0, 0)
 
 
 def kernel(
     zs_n, ys_n, total_rows, ratio, m_ref, g_ref, q_ref, update_ref, momentum_ref, left_ref, basis_ref,
-    part, ybuf, chunks, raw, gpart, gcbuf, gxsum, gxbuf, gzsum, gzbuf, gfull,
+    part, ybuf, ysum, chunks, raw, gpart, gcbuf, gxsum, gxbuf, gzsum, gzbuf, gfull,
     wpart, wcbuf, wxsum, wxbuf, wzsum, wzbuf, wfull, work, top, right, norms,
     s_y, r_y, s_y2, r_y2, s_n, r_n,
     s_hc, r_hc, s_hx, r_hx, s_hz, r_hz, s_gy, r_gy, s_gx, r_gx, s_gc, r_gc,
@@ -142,7 +151,8 @@
     z, x, core, y = place()
     half = part.shape[1]
     lanes = part.shape[2]
-    across = raw.shape[1] // lanes
+    rank = raw.shape[1]
+    across = rank // lanes
 
     def send(src, dst, ssem, rsem, to):
         pltpu.make_async_remote_copy(
@@ -194,12 +204,49 @@
         part[k] = left_part[row * half : (row + 1) * half, col * lanes : (col + 1) * lanes]
     pl.semaphore_wait(barrier, (ys_n - 1) + 1 + (XS - 1) + (zs_n - 1))
 
-    each(1, ys_n, lambda d: send(part.at[y_of(d)], ybuf.at[y], s_y.at[d], r_y.at[y], at_y(y_of(d))))
-    ybuf[y] = part[y]
-    each(1, ys_n, lambda d: done(ybuf.at[y_of(d)], r_y.at[y_of(d)]))
-    chunks[y] = total(ybuf)
-    each(1, ys_n, lambda d: send(chunks.at[y], chunks.at[y], s_y2.at[d], r_y2.at[y], at_y(y_of(d))))
-    each(1, ys_n, lambda d: done(chunks.at[y_of(d)], r_y2.at[y_of(d)]))
+    ways = ((1, ys_n // 2), (-1, (ys_n - 1) // 2))
+    most = ways[0][1]
+    cut = half // 16 * 8 + 8
+    pieces = (slice(0, cut), slice(cut, half))
+
+    def slot(way, step):
+        return way * most + step - 1
+
+    def sem(way, step, piece):
+        return slot(way, step) * len(pieces) + piece
+
+    def hops():
+        for step in range(1, most + 1):
+            for piece, rows in enumerate(pieces):
+                for way, (sign, steps) in enumerate(ways):
+                    if step <= steps:
+                        yield step, piece, rows, way, sign, steps
+
+    for step, piece, rows, way, sign, steps in hops():
+        to = (y + sign * (steps + 1 - step) + ys_n) % ys_n
+        out = part.at[to, rows]
+        if step > 1:
+            came = slot(way, step - 1)
+            done(ybuf.at[came, rows], r_y.at[sem(way, step - 1, piece)])
+            ysum[came + 1, rows] = ybuf[came, rows] + part[to, rows]
+            out = ysum.at[came + 1, rows]
+        k = sem(way, step, piece)
+        send(out, ybuf.at[slot(way, step), rows], s_y.at[k], r_y.at[k], at_y((y + sign + ys_n) % ys_n))
+    for piece, rows in enumerate(pieces):
+        acc = part[y, rows]
+        for way, (sign, steps) in enumerate(ways):
+            done(ybuf.at[slot(way, steps), rows], r_y.at[sem(way, steps, piece)])
+            acc = acc + ybuf[slot(way, steps), rows]
+        chunks[y, rows] = acc
+    for step, piece, rows, way, sign, steps in hops():
+        block = chunks.at[(y - sign * (step - 1) + ys_n) % ys_n, rows]
+        if step > 1:
+            done(block, r_y2.at[sem(way, step - 1, piece)])
+        k = sem(way, step, piece)
+        send(block, block, s_y2.at[k], r_y2.at[k], at_y((y + sign + ys_n) % ys_n))
+    for piece, rows in enumerate(pieces):
+        for way, (sign, steps) in enumerate(ways):
+            done(chunks.at[(y - sign * steps + ys_n) % ys_n, rows], r_y2.at[sem(way, steps, piece)])
     for k in range(ys_n):
         row, col = k // across, k % across
         raw[row * half : (row + 1) * half, col * lanes : (col + 1) * lanes] = chunks[k]
@@ -212,12 +259,16 @@
     send(ghalf, gcbuf, s_hc, r_hc, partner)
 
     wpart[...] = dot3(summed, split(raw[...]), 0, 0).reshape(wpart.shape)
-    each(1, XS + 1, lambda d: send(
-        wpart.at[:, x_of(d), 1 - core], wcbuf.at[x_of(d)], s_c.at[d - 1], r_c.at[x_of(d)], partner))
+
+    def w_across(d):
+        send(wpart.at[:, x_of(d), 1 - core], wcbuf.at[x_of(d)], s_c.at[d], r_c.at[x_of(d)], partner)
+
+    each_peer(XS, w_across)
+    w_across(0)
 
     done(gcbuf, r_hc)
     gxsum[...] = gpart[plane, :, core] + gcbuf[...]
-    each(1, XS, lambda d: send(gxsum.at[x_of(d)], gxbuf.at[x], s_hx.at[d], r_hx.at[x], at_x(x_of(d))))
+    each_peer(XS, lambda d: send(gxsum.at[x_of(d)], gxbuf.at[x], s_hx.at[d], r_hx.at[x], at_x(x_of(d))))
     gxbuf[x] = gxsum[x]
 
     def w_forward(d):
@@ -226,10 +277,10 @@
         wxsum[k] = wpart[:, k, core] + wcbuf[k]
         send(wxsum.at[k], wxbuf.at[x], s_x.at[d], r_x.at[x], at_x(k))
 
-    each(1, XS, w_forward)
+    each_peer(XS, w_forward)
     each(1, XS, lambda d: done(gxbuf.at[x_of(d)], r_hx.at[x_of(d)]))
     gzsum[...] = total(gxbuf)
-    each(1, zs_n, lambda d: send(gzsum, gzbuf.at[z], s_hz.at[d], r_hz.at[z], at_z(z_of(d))))
+    each_peer(zs_n, lambda d: send(gzsum, gzbuf.at[z], s_hz.at[d], r_hz.at[z], at_z(z_of(d))))
     gzbuf[z] = gzsum[...]
     done(wcbuf.at[x], r_c.at[x])
     wxbuf[x] = wpart[:, x, core] + wcbuf[x]
@@ -237,26 +288,44 @@
     each(1, zs_n, lambda d: done(gzbuf.at[z_of(d)], r_hz.at[z_of(d)]))
     gfull[y, x, core] = total(gzbuf)
     gown = gfull.at[y, x, core]
-    each(1, ys_n, lambda d: send(gown, gown, s_gy.at[d], r_gy.at[y], at_y(y_of(d))))
+    each_peer(ys_n, lambda d: send(gown, gown, s_gy.at[d], r_gy.at[y], at_y(y_of(d))))
 
     each(1, XS, lambda d: done(wxbuf.at[x_of(d)], r_x.at[x_of(d)]))
     wzsum[...] = total(wxbuf)
-    each(1, zs_n, lambda d: send(wzsum.at[z_of(d)], wzbuf.at[z], s_z.at[d], r_z.at[z], at_z(z_of(d))))
+    each_peer(zs_n, lambda d: send(wzsum.at[z_of(d)], wzbuf.at[z], s_z.at[d], r_z.at[z], at_z(z_of(d))))
     wzbuf[z] = wzsum[z]
 
     each(1, ys_n, lambda d: done(gfull.at[y_of(d), x, core], r_gy.at[y_of(d)]))
-    gx = gfull.at[:, x, core]
-    each(1, XS, lambda d: send(gx, gx, s_gx.at[d], r_gx.at[x], at_x(x_of(d))))
-    each(1, XS, lambda d: done(gfull.at[:, x_of(d), core], r_gx.at[x_of(d)]))
-    gc = gfull.at[:, :, core]
-    send(gc, gc, s_gc, r_gc, partner)
-    done(gfull.at[:, :, 1 - core], r_gc)
-    work[...] = gfull[...].reshape(work.shape)
+    blocks = range(rank // lanes)
+
+    def upper(block, *at):
+        return gfull.at[(slice(0, per * (block + 1)), *at, slice(None), slice(block * lanes, (block + 1) * lanes))]
+
+    def gather_x(d):
+        for k in blocks:
+            mine = upper(k, x, core)
+            send(mine, mine, s_gx.at[d * len(blocks) + k], r_gx.at[x * len(blocks) + k], at_x(x_of(d)))
+
+    def gathered_x(d):
+        for k in blocks:
+            done(upper(k, x_of(d), core), r_gx.at[x_of(d) * len(blocks) + k])
+
+    each_peer(XS, gather_x)
+    each(1, XS, gathered_x)
+    for k in blocks:
+        send(upper(k, slice(None), core), upper(k, slice(None), core), s_gc.at[k], r_gc.at[k], partner)
+    for k in blocks:
+        done(upper(k, slice(None), 1 - core), r_gc.at[k])
+        end = (k + 1) * lanes
+        here = slice(k * lanes, end)
+        work[0:end, here] = gfull[0 : per * (k + 1), :, :, :, here].reshape(end, lanes)
+        if end < rank:
+            work[end:, here] = jnp.zeros((rank - end, lanes), jnp.float32)
 
     each(1, zs_n, lambda d: done(wzbuf.at[z_of(d)], r_z.at[z_of(d)]))
     wfull[z, x, core] = total(wzbuf)
     wown = wfull.at[z, x, core]
-    each(1, zs_n, lambda d: send(wown, wown, s_wz.at[d], r_wz.at[z], at_z(z_of(d))))
+    each_peer(zs_n, lambda d: send(wown, wown, s_wz.at[d], r_wz.at[z], at_z(z_of(d))))
     wx = wfull.at[:, x, core]
     wc = wfull.at[:, :, core]
 
@@ -266,7 +335,7 @@
             @pl.when(b == 0)
             def _():
                 each(1, zs_n, lambda d: done(wfull.at[z_of(d), x, core], r_wz.at[z_of(d)]))
-                each(1, XS, lambda d: send(wx, wx, s_wx.at[d], r_wx.at[x], at_x(x_of(d))))
+                each_peer(XS, lambda d: send(wx, wx, s_wx.at[d], r_wx.at[x], at_x(x_of(d))))
 
             @pl.when(b == 2)
             def _():
@@ -281,27 +350,26 @@
     right[...] = dot3(split(wfull[...].reshape(right.shape)), inverse, 1, 1)
     values = right[...]
     norms[y] = jnp.sum(values * values, axis=0, keepdims=True)
-    each(1, ys_n, lambda d: send(norms.at[y], norms.at[y], s_n.at[d], r_n.at[y], at_y(y_of(d))))
-    rows = split(values)
+    each_peer(ys_n, lambda d: send(norms.at[y], norms.at[y], s_n.at[d], r_n.at[y], at_y(y_of(d))))
+    right_parts = split(values)
     left = dot3(split(raw[...]), inverse, 1, 1)
     left_ref[...] = left * math.sqrt(total_rows)
-    product = dot3(split(left), rows, 1, 1)
+    product = dot3(split(left), right_parts, 1, 1)
     momentum_ref[...] = (m_ref[...] + g_ref[...].astype(jnp.float32)) - 0.5 * product
     each(1, ys_n, lambda d: done(norms.at[y_of(d)], r_n.at[y_of(d)]))
     column_norm = jnp.sqrt(total(norms) + EPSILON)
-    update_ref[...] = dot3(split(left * (ratio / column_norm)), rows, 1, 1).astype(update_ref.dtype)
+    update_ref[...] = dot3(split(left * (ratio / column_norm)), right_parts, 1, 1).astype(update_ref.dtype)
     me = pl.multiple_of(lax.axis_index("fsdp") * 8, 8)
     basis_ref[...] = right[pl.ds(me, 8), :] / column_norm
 
     def sent_y(d):
-        done(part.at[y_of(d)], s_y.at[d])
-        done(chunks.at[y], s_y2.at[d])
         done(gown, s_gy.at[d])
         done(norms.at[y], s_n.at[d])
 
     def sent_x(d):
         done(gxsum.at[x_of(d)], s_hx.at[d])
-        done(gx, s_gx.at[d])
+        for k in blocks:
+            done(upper(k, x, core), s_gx.at[d * len(blocks) + k])
         done(wxsum.at[x_of(d)], s_x.at[d])
         done(wx, s_wx.at[d])
 
@@ -313,9 +381,14 @@
     each(1, ys_n, sent_y)
     each(1, XS, sent_x)
     each(1, zs_n, sent_z)
-    each(1, XS + 1, lambda d: done(wpart.at[:, x_of(d), 1 - core], s_c.at[d - 1]))
+    each(0, XS, lambda d: done(wpart.at[:, x_of(d), 1 - core], s_c.at[d]))
     done(ghalf, s_hc)
-    done(gc, s_gc)
+    for k in blocks:
+        done(upper(k, slice(None), core), s_gc.at[k])
+    for step, piece, rows, way, sign, steps in hops():
+        k = sem(way, step, piece)
+        done(part.at[y, rows], s_y.at[k])
+        done(chunks.at[y, rows], s_y2.at[k])
     done(wc, s_wc)
 
 
@@ -355,14 +428,15 @@
         in_specs=[vmem] * 3,
         out_specs=(vmem,) * 4,
         scratch_shapes=[
-            buffer(ys_n, half, lanes), buffer(ys_n, half, lanes), buffer(ys_n, half, lanes), buffer(rows, rank),
+            buffer(ys_n, half, lanes), buffer(ys_n, half, lanes), buffer(ys_n, half, lanes), buffer(ys_n, half, lanes),
+            buffer(rows, rank),
             buffer(per, XS, CORES, 8, rank), gsum, gsum, gsum, buffer(8, rank), buffer(zs_n, 8, rank),
             buffer(ys_n, XS, CORES, 8, rank),
             buffer(zs_n, XS, CORES, 8, rank), wsum, wsum, wsum, buffer(zs_n, 8, rank), buffer(zs_n, 8, rank),
             buffer(zs_n, XS, CORES, 8, rank),
             buffer(rank, rank), buffer(BLOCK, BLOCK), buffer(cols, rank), buffer(ys_n, 1, rank),
-            *sems(ys_n), *sems(ys_n), *sems(ys_n),
-            *one, *sems(XS), *sems(zs_n), *sems(ys_n), *sems(XS), *one,
+            *sems(2 * ys_n), *sems(2 * ys_n), *sems(ys_n),
+            *one, *sems(XS), *sems(zs_n), *sems(ys_n), *sems(XS * rank // lanes), *sems(rank // lanes),
             *sems(XS), *sems(XS), *sems(zs_n), *sems(zs_n), *sems(XS), *one,
         ],
         compiler_params=pltpu.CompilerParams(

time: 121 us -> 112 us (0.926)
  Pallas kernels: 115 us -> 105 us
  local copies, waits for them, and re-layouts: 5.22 us -> 6.49 us
    pallas_call x1, Pallas kernels: 115 us -> 105 us  [on_device(): pl.pallas_call(functools.partial(kernel, zs_n, ys_n, total_rows, ratio),...]
    unnamed x8 -> x10, local copies, waits for them, and re-layouts: 5.22 us -> 6.49 us
where the time goes in v3:
time: 112 us
  Pallas kernels  105 us (94%)
  local copies, waits for them, and re-layouts  6.49 us (6%)
    pallas_call x1, Pallas kernels, on_device(): pl.pallas_call(functools.partial(kernel, zs_n, ys_n, total_rows, ratio),...  105 us
    unnamed x10, local copies, waits for them, and re-layouts  6.49 us

profile of v3, /device:TPU:1, one launch (start us, length us, event | category | flops | bytes accessed | tf_op | source)
XLA Modules:
  0.0 111.9 jit_solution(4146494992234687393)
XLA Ops:
  0.6 0.0 copy-start
  0.6 1.4 %copy-done = f32[768,512]{1,0:T(8,128)S(1)} copy-done((f32[768,512]{1,0:T(8,128)S(1)}, f32[768,512]{1,0:T(8,128)}, u32[]{:S(2)}) %copy-start) | copy-done | bytes 1572888
  2.0 0.0 copy-start.1
  2.0 1.1 copy-done.1
  3.2 0.0 copy-start.2
  3.2 1.0 copy-done.2
  4.1 104.7 %step.1 = (bf16[240,768]{1,0:T(8,128)(2,1)S(1)}, f32[240,768]{1,0:T(8,128)S(1)}, f32[240,512]{1,0:T(8,128)S(1)}, f32[8,512]{1,0:T(8,128)S(1)}) custom-call(f32[240,768]{1,0:T(8,128)S(1)} %copy-done.1, bf16[240,768]{1,0:T(8,128)(2,1)S(1)} %copy-done.2, f32[768,512]{1,0:T(8,128)S(1)} %copy-done), custom_call_target="tpu_custom_call" | custom-call | tf_op jit(solution)/shard_map/step/pallas_call | solution.py:419
  108.9 0.7 copy.11
  109.6 0.9 copy.12
  110.5 0.8 copy.13
  111.3 0.6 copy.14
Async XLA Ops:
  0.6 1.4 %copy-start = (f32[768,512]{1,0:T(8,128)S(1)}, f32[768,512]{1,0:T(8,128)}, u32[]{:S(2)}) copy-start(f32[768,512]{1,0:T(8,128)} %q_ref.1) | copy-start | bytes 4718596
  2.0 1.1 copy-start.1
  3.2 1.0 copy-start.2

commit v4 on v3

--- a/solution.py
+++ b/solution.py
@@ -51,18 +51,15 @@
     lax.fori_loop(start, stop, step, 0)
 
 
-def each_peer(count, body):
-    def step(k):
-        off = (k + 1) // 2
-        body(count // 2 + off * (1 - 2 * (k % 2)))
-
-    each(0, count - 1, step)
+def far_first(count):
+    return sorted(range(1, count), key=lambda d: -min(d, count - d))
 
 
 BLOCK = 128
-
-
-def factor_block(tiles):
+GROUP, NEAR = 4, 1
+
+
+def factor_block(tiles, panel_ref):
     shape = (8, BLOCK)
     lane = lax.broadcasted_iota(jnp.int32, shape, 1)
     sub = lax.broadcasted_iota(jnp.int32, shape, 0)
@@ -78,6 +75,9 @@
     tiles = list(tiles)
     for t in range(count):
         base = 8 * t
+        first = t // GROUP * GROUP
+        end = first + GROUP
+        near = min(end + NEAR, count)
         here = (lane >= base) & (lane < base + 8)
         tile = tiles[t]
         cols = [column(tile, base + c) for c in range(8)]
@@ -98,6 +98,7 @@
         for p in range(7):
             done = jnp.where(sub == p, rows[p], done)
         out.append(jnp.where(lane < base + 8, done, 0.0))
+        panel_ref[base - 8 * first : base - 8 * first + 8, :] = jnp.where((lane < base + 8) | (lane >= 8 * end), done, 0.0)
         if t + 1 == count:
             break
         solved = [None] * 8
@@ -106,20 +107,27 @@
             for q in reversed(range(p + 1, 8)):
                 w = w - low[p, q] * solved[q]
             solved[p] = w * scale[p]
-        for i in range(t + 1, count):
+        for i in range(t + 1, near):
             acc = jnp.where(here, 0.0, tiles[i])
             for p in reversed(range(8)):
                 acc = acc - column(tiles[i], base + p) * solved[p]
             tiles[i] = acc
+        if t + 1 == end and near < count:
+            panel = panel_ref[...]
+            low = jnp.where(lax.broadcasted_iota(jnp.int32, panel.shape, 1) >= 8 * near, panel, 0.0)
+            change = dot3(split(low), split(panel), 0, 0)
+            gone = (lane >= 8 * first) & (lane < 8 * end)
+            for i in range(near, count):
+                tiles[i] = jnp.where(gone, 0.0, tiles[i]) - change[8 * i : 8 * i + 8]
     return out
 
 
-def factor_step(b, work, top_ref, between):
+def factor_step(b, work, top_ref, panel_ref, between):
     size = work.shape[0]
     off = pl.multiple_of(b * BLOCK, BLOCK)
     here = pl.ds(off, BLOCK)
     tiles = [work[pl.ds(pl.multiple_of(off + 8 * i, 8), 8), here] for i in range(BLOCK // 8)]
-    for i, tile in enumerate(factor_block(tiles)):
+    for i, tile in enumerate(factor_block(tiles, panel_ref)):
         top_ref[8 * i : 8 * i + 8, :] = tile
     between()
     lane = lax.broadcasted_iota(jnp.int32, (BLOCK, size), 1)
@@ -141,13 +149,19 @@
 
 
 def kernel(
-    zs_n, ys_n, total_rows, ratio, m_ref, g_ref, q_ref, update_ref, momentum_ref, left_ref, basis_ref,
-    part, ybuf, ysum, chunks, raw, gpart, gcbuf, gxsum, gxbuf, gzsum, gzbuf, gfull,
-    wpart, wcbuf, wxsum, wxbuf, wzsum, wzbuf, wfull, work, top, right, norms,
+    zs_n, ys_n, total_rows, ratio, m_hbm, g_hbm, q_hbm, update_ref, momentum_ref, left_ref, basis_ref,
+    m_ref, g_ref, q_ref, s_in, part, ybuf, ysum, chunks, raw, gpart, gcbuf, gxsum, gxbuf, gzsum, gzbuf, gfull,
+    wpart, wcbuf, wxsum, wxbuf, wzsum, wzbuf, wfull, work, top, panel, right, norms,
     s_y, r_y, s_y2, r_y2, s_n, r_n,
     s_hc, r_hc, s_hx, r_hx, s_hz, r_hz, s_gy, r_gy, s_gx, r_gx, s_gc, r_gc,
     s_c, r_c, s_x, r_x, s_z, r_z, s_wz, r_wz, s_wx, r_wx, s_wc, r_wc,
 ):
+    loads = [
+        pltpu.make_async_copy(src, dst, s_in.at[k])
+        for k, (src, dst) in enumerate(((q_hbm, q_ref), (m_hbm, m_ref), (g_hbm, g_ref)))
+    ]
+    for load in loads:
+        load.start()
     z, x, core, y = place()
     half = part.shape[1]
     lanes = part.shape[2]
@@ -168,14 +182,11 @@
             acc = acc + ref[k]
         return acc
 
-    def x_of(d):
-        return (x + d) % XS
-
-    def y_of(d):
-        return (y + d) % ys_n
-
-    def z_of(d):
-        return (z + d) % zs_n
+    def ring(at, count):
+        known = [at] + [lax.rem(at + d, count) for d in range(1, count)]
+        return lambda d: known[d] if isinstance(d, int) else lax.rem(at + d, count)
+
+    x_of, y_of, z_of = ring(x, XS), ring(y, ys_n), ring(z, zs_n)
 
     def at_x(k):
         return device(z, k, core, y)
@@ -197,7 +208,10 @@
     each(1, XS, lambda d: greet(at_x(x_of(d))))
     each(1, zs_n, lambda d: greet(at_z(z_of(d))))
 
-    summed = split(m_ref[...] + g_ref[...].astype(jnp.float32))
+    for load in loads:
+        load.wait()
+    m_ref[...] = m_ref[...] + g_ref[...].astype(jnp.float32)
+    summed = split(m_ref[...])
     left_part = dot3(summed, split(q_ref[...]))
     for k in range(ys_n):
         row, col = k // across, k % across
@@ -220,10 +234,10 @@
             for piece, rows in enumerate(pieces):
                 for way, (sign, steps) in enumerate(ways):
                     if step <= steps:
-                        yield step, piece, rows, way, sign, steps
+                        yield step, piece, rows, way, sign * (1 - 2 * piece), steps
 
     for step, piece, rows, way, sign, steps in hops():
-        to = (y + sign * (steps + 1 - step) + ys_n) % ys_n
+        to = y_of((sign * (steps + 1 - step)) % ys_n)
         out = part.at[to, rows]
         if step > 1:
             came = slot(way, step - 1)
@@ -231,7 +245,7 @@
             ysum[came + 1, rows] = ybuf[came, rows] + part[to, rows]
             out = ysum.at[came + 1, rows]
         k = sem(way, step, piece)
-        send(out, ybuf.at[slot(way, step), rows], s_y.at[k], r_y.at[k], at_y((y + sign + ys_n) % ys_n))
+        send(out, ybuf.at[slot(way, step), rows], s_y.at[k], r_y.at[k], at_y(y_of(sign % ys_n)))
     for piece, rows in enumerate(pieces):
         acc = part[y, rows]
         for way, (sign, steps) in enumerate(ways):
@@ -239,14 +253,14 @@
             acc = acc + ybuf[slot(way, steps), rows]
         chunks[y, rows] = acc
     for step, piece, rows, way, sign, steps in hops():
-        block = chunks.at[(y - sign * (step - 1) + ys_n) % ys_n, rows]
+        block = chunks.at[y_of((-sign * (step - 1)) % ys_n), rows]
         if step > 1:
             done(block, r_y2.at[sem(way, step - 1, piece)])
         k = sem(way, step, piece)
-        send(block, block, s_y2.at[k], r_y2.at[k], at_y((y + sign + ys_n) % ys_n))
+        send(block, block, s_y2.at[k], r_y2.at[k], at_y(y_of(sign % ys_n)))
     for piece, rows in enumerate(pieces):
         for way, (sign, steps) in enumerate(ways):
-            done(chunks.at[(y - sign * steps + ys_n) % ys_n, rows], r_y2.at[sem(way, steps, piece)])
+            done(chunks.at[y_of((-sign * (1 - 2 * piece) * steps) % ys_n), rows], r_y2.at[sem(way, steps, piece)])
     for k in range(ys_n):
         row, col = k // across, k % across
         raw[row * half : (row + 1) * half, col * lanes : (col + 1) * lanes] = chunks[k]
@@ -263,12 +277,14 @@
     def w_across(d):
         send(wpart.at[:, x_of(d), 1 - core], wcbuf.at[x_of(d)], s_c.at[d], r_c.at[x_of(d)], partner)
 
-    each_peer(XS, w_across)
+    for d in far_first(XS):
+        w_across(d)
     w_across(0)
 
     done(gcbuf, r_hc)
     gxsum[...] = gpart[plane, :, core] + gcbuf[...]
-    each_peer(XS, lambda d: send(gxsum.at[x_of(d)], gxbuf.at[x], s_hx.at[d], r_hx.at[x], at_x(x_of(d))))
+    for d in far_first(XS):
+        send(gxsum.at[x_of(d)], gxbuf.at[x], s_hx.at[d], r_hx.at[x], at_x(x_of(d)))
     gxbuf[x] = gxsum[x]
 
     def w_forward(d):
@@ -277,25 +293,33 @@
         wxsum[k] = wpart[:, k, core] + wcbuf[k]
         send(wxsum.at[k], wxbuf.at[x], s_x.at[d], r_x.at[x], at_x(k))
 
-    each_peer(XS, w_forward)
-    each(1, XS, lambda d: done(gxbuf.at[x_of(d)], r_hx.at[x_of(d)]))
+    for d in far_first(XS):
+        w_forward(d)
+    for d in range(1, XS):
+        done(gxbuf.at[x_of(d)], r_hx.at[x_of(d)])
     gzsum[...] = total(gxbuf)
-    each_peer(zs_n, lambda d: send(gzsum, gzbuf.at[z], s_hz.at[d], r_hz.at[z], at_z(z_of(d))))
+    for d in far_first(zs_n):
+        send(gzsum, gzbuf.at[z], s_hz.at[d], r_hz.at[z], at_z(z_of(d)))
     gzbuf[z] = gzsum[...]
     done(wcbuf.at[x], r_c.at[x])
     wxbuf[x] = wpart[:, x, core] + wcbuf[x]
 
-    each(1, zs_n, lambda d: done(gzbuf.at[z_of(d)], r_hz.at[z_of(d)]))
+    for d in range(1, zs_n):
+        done(gzbuf.at[z_of(d)], r_hz.at[z_of(d)])
     gfull[y, x, core] = total(gzbuf)
     gown = gfull.at[y, x, core]
-    each_peer(ys_n, lambda d: send(gown, gown, s_gy.at[d], r_gy.at[y], at_y(y_of(d))))
-
-    each(1, XS, lambda d: done(wxbuf.at[x_of(d)], r_x.at[x_of(d)]))
+    for d in far_first(ys_n):
+        send(gown, gown, s_gy.at[d], r_gy.at[y], at_y(y_of(d)))
+
+    for d in range(1, XS):
+        done(wxbuf.at[x_of(d)], r_x.at[x_of(d)])
     wzsum[...] = total(wxbuf)
-    each_peer(zs_n, lambda d: send(wzsum.at[z_of(d)], wzbuf.at[z], s_z.at[d], r_z.at[z], at_z(z_of(d))))
+    for d in far_first(zs_n):
+        send(wzsum.at[z_of(d)], wzbuf.at[z], s_z.at[d], r_z.at[z], at_z(z_of(d)))
     wzbuf[z] = wzsum[z]
 
-    each(1, ys_n, lambda d: done(gfull.at[y_of(d), x, core], r_gy.at[y_of(d)]))
+    for d in range(1, ys_n):
+        done(gfull.at[y_of(d), x, core], r_gy.at[y_of(d)])
     blocks = range(rank // lanes)
 
     def upper(block, *at):
@@ -310,10 +334,18 @@
         for k in blocks:
             done(upper(k, x_of(d), core), r_gx.at[x_of(d) * len(blocks) + k])
 
-    each_peer(XS, gather_x)
-    each(1, XS, gathered_x)
+    for d in far_first(XS):
+        gather_x(d)
+    for d in range(1, XS):
+        gathered_x(d)
     for k in blocks:
         send(upper(k, slice(None), core), upper(k, slice(None), core), s_gc.at[k], r_gc.at[k], partner)
+    for d in range(1, zs_n):
+        done(wzbuf.at[z_of(d)], r_z.at[z_of(d)])
+    wfull[z, x, core] = total(wzbuf)
+    wown = wfull.at[z, x, core]
+    for d in far_first(zs_n):
+        send(wown, wown, s_wz.at[d], r_wz.at[z], at_z(z_of(d)))
     for k in blocks:
         done(upper(k, slice(None), 1 - core), r_gc.at[k])
         end = (k + 1) * lanes
@@ -322,41 +354,58 @@
         if end < rank:
             work[end:, here] = jnp.zeros((rank - end, lanes), jnp.float32)
 
-    each(1, zs_n, lambda d: done(wzbuf.at[z_of(d)], r_z.at[z_of(d)]))
-    wfull[z, x, core] = total(wzbuf)
-    wown = wfull.at[z, x, core]
-    each_peer(zs_n, lambda d: send(wown, wown, s_wz.at[d], r_wz.at[z], at_z(z_of(d))))
-    wx = wfull.at[:, x, core]
-    wc = wfull.at[:, :, core]
+    cutz = zs_n // 2
+    halves = (slice(0, cutz), slice(cutz, zs_n))
+
+    def w_at(k, zs=slice(None)):
+        return wfull.at[zs, k, core]
+
+    def w_core(k):
+        send(w_at(k), w_at(k), s_wc.at[k], r_wc.at[k], partner)
+
+    def w_start():
+        for d in range(1, zs_n):
+            done(wfull.at[z_of(d), x, core], r_wz.at[z_of(d)])
+        send(w_at(x), w_at(x), s_wx.at[0], r_wx.at[0], at_x(x_of(1)))
+        send(w_at(x), w_at(x), s_wx.at[1], r_wx.at[1], at_x(x_of(XS - 1)))
+        w_core(x)
+
+    def w_relay():
+        behind, ahead = w_at(x_of(XS - 1), halves[0]), w_at(x_of(1), halves[1])
+        done(w_at(x_of(XS - 1)), r_wx.at[0])
+        send(behind, behind, s_wx.at[2], r_wx.at[2], at_x(x_of(1)))
+        done(w_at(x_of(1)), r_wx.at[1])
+        send(ahead, ahead, s_wx.at[3], r_wx.at[3], at_x(x_of(XS - 1)))
+        w_core(x_of(1))
+        w_core(x_of(XS - 1))
 
     @pl.loop(0, work.shape[0] // BLOCK)
     def _(b):
         def between():
-            @pl.when(b == 0)
-            def _():
-                each(1, zs_n, lambda d: done(wfull.at[z_of(d), x, core], r_wz.at[z_of(d)]))
-                each_peer(XS, lambda d: send(wx, wx, s_wx.at[d], r_wx.at[x], at_x(x_of(d))))
-
-            @pl.when(b == 2)
-            def _():
-                each(1, XS, lambda d: done(wfull.at[:, x_of(d), core], r_wx.at[x_of(d)]))
-                send(wc, wc, s_wc, r_wc, partner)
-
-        factor_step(b, work, top, between)
-
-    done(wfull.at[:, :, 1 - core], r_wc)
+            pl.when(b == 1)(w_start)
+            pl.when(b == 2)(w_relay)
+
+        factor_step(b, work, top, panel, between)
+
+    for k, zs in enumerate(halves):
+        done(w_at(x_of(2), zs), r_wx.at[2 + k])
+    w_core(x_of(2))
 
     inverse = split(work[...])
+    left = dot3(split(raw[...]), inverse, 1, 1)
+    left_ref[...] = left * math.sqrt(total_rows)
+    for d in range(XS):
+        done(wfull.at[:, x_of(d), 1 - core], r_wc.at[x_of(d)])
     right[...] = dot3(split(wfull[...].reshape(right.shape)), inverse, 1, 1)
     values = right[...]
     norms[y] = jnp.sum(values * values, axis=0, keepdims=True)
-    each_peer(ys_n, lambda d: send(norms.at[y], norms.at[y], s_n.at[d], r_n.at[y], at_y(y_of(d))))
+    for d in far_first(ys_n):
+        send(norms.at[y], norms.at[y], s_n.at[d], r_n.at[y], at_y(y_of(d)))
     right_parts = split(values)
-    left = dot3(split(raw[...]), inverse, 1, 1)
-    left_ref[...] = left * math.sqrt(total_rows)
     product = dot3(split(left), right_parts, 1, 1)
-    momentum_ref[...] = (m_ref[...] + g_ref[...].astype(jnp.float32)) - 0.5 * product
-    each(1, ys_n, lambda d: done(norms.at[y_of(d)], r_n.at[y_of(d)]))
+    momentum_ref[...] = m_ref[...] - 0.5 * product
+    for d in range(1, ys_n):
+        done(norms.at[y_of(d)], r_n.at[y_of(d)])
     column_norm = jnp.sqrt(total(norms) + EPSILON)
     update_ref[...] = dot3(split(left * (ratio / column_norm)), right_parts, 1, 1).astype(update_ref.dtype)
     me = pl.multiple_of(lax.axis_index("fsdp") * 8, 8)
@@ -371,7 +420,6 @@
         for k in blocks:
             done(upper(k, x, core), s_gx.at[d * len(blocks) + k])
         done(wxsum.at[x_of(d)], s_x.at[d])
-        done(wx, s_wx.at[d])
 
     def sent_z(d):
         done(gzsum, s_hz.at[d])
@@ -389,7 +437,9 @@
         k = sem(way, step, piece)
         done(part.at[y, rows], s_y.at[k])
         done(chunks.at[y, rows], s_y2.at[k])
-    done(wc, s_wc)
+    for k in range(XS):
+        done(w_at(x) if k < 2 else w_at(x, halves[k - 2]), s_wx.at[k])
+        done(w_at(k), s_wc.at[k])
 
 
 def on_device(momentum, gradient, right_basis):
@@ -425,19 +475,20 @@
             jax.ShapeDtypeStruct((rows, rank), f32),
             jax.ShapeDtypeStruct((8, rank), f32),
         ),
-        in_specs=[vmem] * 3,
+        in_specs=[pl.BlockSpec(memory_space=pltpu.HBM)] * 3,
         out_specs=(vmem,) * 4,
         scratch_shapes=[
+            buffer(rows, cols), pltpu.VMEM((rows, cols), jnp.bfloat16), buffer(cols, rank), pltpu.SemaphoreType.DMA((3,)),
             buffer(ys_n, half, lanes), buffer(ys_n, half, lanes), buffer(ys_n, half, lanes), buffer(ys_n, half, lanes),
             buffer(rows, rank),
             buffer(per, XS, CORES, 8, rank), gsum, gsum, gsum, buffer(8, rank), buffer(zs_n, 8, rank),
             buffer(ys_n, XS, CORES, 8, rank),
             buffer(zs_n, XS, CORES, 8, rank), wsum, wsum, wsum, buffer(zs_n, 8, rank), buffer(zs_n, 8, rank),
             buffer(zs_n, XS, CORES, 8, rank),
-            buffer(rank, rank), buffer(BLOCK, BLOCK), buffer(cols, rank), buffer(ys_n, 1, rank),
+            buffer(rank, rank), buffer(BLOCK, BLOCK), buffer(8 * GROUP, BLOCK), buffer(cols, rank), buffer(ys_n, 1, rank),
             *sems(2 * ys_n), *sems(2 * ys_n), *sems(ys_n),
             *one, *sems(XS), *sems(zs_n), *sems(ys_n), *sems(XS * rank // lanes), *sems(rank // lanes),
-            *sems(XS), *sems(XS), *sems(zs_n), *sems(zs_n), *sems(XS), *one,
+            *sems(XS), *sems(XS), *sems(zs_n), *sems(zs_n), *sems(XS), *sems(XS),
         ],
         compiler_params=pltpu.CompilerParams(
             collective_id=0, has_side_effects=True, vmem_limit_bytes=VMEM_LIMIT

time: 112 us -> 111 us (level)
  Pallas kernels: 105 us -> 103 us
    pallas_call x1, Pallas kernels: 105 us -> 103 us  [on_device(): pl.pallas_call(functools.partial(kernel, zs_n, ys_n, total_rows, ratio),...]
where the time goes in v4:
time: 111 us
  Pallas kernels  103 us (93%)
  local copies, waits for them, and re-layouts  6.49 us (6%)
    pallas_call x1, Pallas kernels, on_device(): pl.pallas_call(functools.partial(kernel, zs_n, ys_n, total_rows, ratio),...  103 us
    unnamed x10, local copies, waits for them, and re-layouts  6.49 us

profile of v4, /device:TPU:1, one launch (start us, length us, event | category | flops | bytes accessed | tf_op | source)
XLA Modules:
  0.0 110.6 jit_solution(8522494951160707902)
XLA Ops:
  0.6 0.0 copy-start
  0.6 1.4 %copy-done = f32[768,512]{1,0:T(8,128)S(1)} copy-done((f32[768,512]{1,0:T(8,128)S(1)}, f32[768,512]{1,0:T(8,128)}, u32[]{:S(2)}) %copy-start) | copy-done | bytes 1572888
  2.0 0.0 copy-start.1
  2.0 1.1 %copy-done.1 = f32[240,768]{1,0:T(8,128)S(1)} copy-done((f32[240,768]{1,0:T(8,128)S(1)}, f32[240,768]{1,0:T(8,128)}, u32[]{:S(2)}) %copy-start.1) | copy-done | bytes 737304
  3.2 0.0 copy-start.2
  3.2 1.0 copy-done.2
  4.1 103.5 %step.1 = (bf16[240,768]{1,0:T(8,128)(2,1)S(1)}, f32[240,768]{1,0:T(8,128)S(1)}, f32[240,512]{1,0:T(8,128)S(1)}, f32[8,512]{1,0:T(8,128)S(1)}) custom-call(f32[240,768]{1,0:T(8,128)S(1)} %copy-done.1, bf16[240,768]{1,0:T(8,128)(2,1)S(1)} %copy-done.2, f32[768,512]{1,0:T(8,128)S(1)} %copy-done), custom_call_target="tpu_custom_call" | custom-call | tf_op jit(solution)/shard_map/step/pallas_call | solution.py:469
  107.6 0.7 copy.11
  108.4 0.9 copy.12
  109.2 0.8 copy.13
  110.0 0.6 copy.14
Async XLA Ops:
  0.6 1.4 %copy-start = (f32[768,512]{1,0:T(8,128)S(1)}, f32[768,512]{1,0:T(8,128)}, u32[]{:S(2)}) copy-start(f32[768,512]{1,0:T(8,128)} %q_hbm.1) | copy-start | bytes 4718596
  2.0 1.1 %copy-start.1 = (f32[240,768]{1,0:T(8,128)S(1)}, f32[240,768]{1,0:T(8,128)}, u32[]{:S(2)}) copy-start(f32[240,768]{1,0:T(8,128)} %m_hbm.1) | copy-start | bytes 2211844
  3.2 1.0 copy-start.2

commit v5 on v4

--- a/solution.py
+++ b/solution.py
@@ -382,11 +382,11 @@
     @pl.loop(0, work.shape[0] // BLOCK)
     def _(b):
         def between():
-            pl.when(b == 1)(w_start)
-            pl.when(b == 2)(w_relay)
+            pl.when(b == 2)(w_start)
 
         factor_step(b, work, top, panel, between)
 
+    w_relay()
     for k, zs in enumerate(halves):
         done(w_at(x_of(2), zs), r_wx.at[2 + k])
     w_core(x_of(2))

time: 111 us -> 112 us (level)
  Pallas kernels: 103 us -> 105 us
    pallas_call x1, Pallas kernels: 103 us -> 105 us  [on_device(): pl.pallas_call(functools.partial(kernel, zs_n, ys_n, total_rows, ratio),...]
where the time goes in v5:
time: 112 us
  Pallas kernels  105 us (94%)
  local copies, waits for them, and re-layouts  6.49 us (6%)
    pallas_call x1, Pallas kernels, on_device(): pl.pallas_call(functools.partial(kernel, zs_n, ys_n, total_rows, ratio),...  105 us
    unnamed x10, local copies, waits for them, and re-layouts  6.49 us

profile of v5, /device:TPU:1, one launch (start us, length us, event | category | flops | bytes accessed | tf_op | source)
XLA Modules:
  0.0 112.2 jit_solution(14488633477044924625)
XLA Ops:
  0.6 0.0 copy-start
  0.6 1.4 %copy-done = f32[768,512]{1,0:T(8,128)S(1)} copy-done((f32[768,512]{1,0:T(8,128)S(1)}, f32[768,512]{1,0:T(8,128)}, u32[]{:S(2)}) %copy-start) | copy-done | bytes 1572888
  2.0 0.0 copy-start.1
  2.0 1.1 copy-done.1
  3.2 0.0 copy-start.2
  3.2 1.0 copy-done.2
  4.1 105.1 %step.1 = (bf16[240,768]{1,0:T(8,128)(2,1)S(1)}, f32[240,768]{1,0:T(8,128)S(1)}, f32[240,512]{1,0:T(8,128)S(1)}, f32[8,512]{1,0:T(8,128)S(1)}) custom-call(f32[240,768]{1,0:T(8,128)S(1)} %copy-done.1, bf16[240,768]{1,0:T(8,128)(2,1)S(1)} %copy-done.2, f32[768,512]{1,0:T(8,128)S(1)} %copy-done), custom_call_target="tpu_custom_call" | custom-call | tf_op jit(solution)/shard_map/step/pallas_call | solution.py:469
  109.2 0.7 copy.11
  110.0 0.9 copy.12
  110.8 0.8 copy.13
  111.6 0.6 copy.14
Async XLA Ops:
  0.6 1.4 %copy-start = (f32[768,512]{1,0:T(8,128)S(1)}, f32[768,512]{1,0:T(8,128)}, u32[]{:S(2)}) copy-start(f32[768,512]{1,0:T(8,128)} %q_hbm.1) | copy-start | bytes 4718596
  2.0 1.1 copy-start.1
  3.2 1.0 copy-start.2
